TPU v7x, 32 devices: a whole 2x2x4 slice. The times are simulated.
32 devices in a mesh: seq: 8 (over y, x, core), tp: 4 (over z).
Axes of the slice: x: 2, y: 2, z: 4, core: 2. Of those that a mesh axis runs over, the one named last changes fastest.
Arguments:
- tokens: bfloat16 [1, 8, 1024, 768], P(None, 'seq', 'tp'), may hold values from -6 to 6
- cotangent: bfloat16 [1, 8, 1024, 768], P(None, 'seq', 'tp'), may hold values from -6 to 6
- lengths: int32 [1], replicated, may hold values from 64 to 1024
- column_mask: int32 [1, 1024], replicated, may hold values 0 or 1
- row_gain: float32 [768], replicated, may hold values from 0.5 to 1.5
- row_qkv: bfloat16 [3, 768, 768], P(None, None, 'tp'), may hold values from -0.3125 to 0.3125
- row_out: bfloat16 [768, 768], P('tp'), may hold values from -0.625 to 0.625
- col_gain: float32 [768], replicated, may hold values from 0.5 to 1.5
- col_qkv: bfloat16 [3, 768, 768], P(None, None, 'tp'), may hold values from -0.21875 to 0.21875
- col_out: bfloat16 [768, 768], P('tp'), may hold values from -0.875 to 0.875
- ffn_gain: float32 [768], replicated, may hold values from 0.5 to 1.5
- ffn_up: bfloat16 [768, 3072], P(None, 'tp'), may hold values from -0.21875 to 0.21875
- ffn_down: bfloat16 [3072, 768], P('tp'), may hold values from -0.109375 to 0.109375
Outputs:
- activations: bfloat16 [1, 8, 1024, 768], P(None, 'seq', 'tp')
- input_grad: bfloat16 [1, 8, 1024, 768], P(None, 'seq', 'tp')
- row_gain_grad: float32 [768], replicated
- row_qkv_grad: float32 [3, 768, 768], P(None, 'seq', 'tp')
- row_out_grad: float32 [768, 768], P('tp', 'seq')
- col_gain_grad: float32 [768], replicated
- col_qkv_grad: float32 [3, 768, 768], P(None, 'seq', 'tp')
- col_out_grad: float32 [768, 768], P('tp', 'seq')
- ffn_gain_grad: float32 [768], replicated
- ffn_up_grad: float32 [768, 3072], P('seq', 'tp')
- ffn_down_grad: float32 [3072, 768], P('tp', 'seq')
All inputs are finite; a program needn't handle non-finite values.
Results may differ from a plain program's by a relative error of at most 0.025.
The roundings to bfloat16 on the way count: a program that leaves them out, or rounds other values in their place, can miss the bound.
Values may be sent and summed in bfloat16 or wider, within the bound.
No kernel may reach another device: no remote copies, remote signals or barrier semaphores. Data moves between devices by JAX's collectives and lax.ppermute only.
A program may use at most 192 MiB of HBM per device.

v0:
```python
import functools

import jax
import jax.numpy as jnp
from jax import lax
from jax.experimental import pallas as pl
from jax.experimental.pallas import tpu as pltpu
from jax.sharding import Mesh
from jax.sharding import PartitionSpec as P

HEADS = 12
HEAD = 64
EPSILON = 1e-05
NEGATIVE = -1e30
ENTROPY_WEIGHT = 4.0

SEQ = ("c", "r")
BF = jnp.bfloat16
F32 = jnp.float32
VMEM_LIMIT = 60 * 1024 * 1024


def statistics(value):
    average = jnp.mean(value, axis=-1, keepdims=True)
    centred = value - average
    inverse = lax.rsqrt(jnp.mean(centred * centred, axis=-1, keepdims=True) + EPSILON)
    return centred * inverse, inverse


def layer_norm(value, gain):
    unit, _ = statistics(value)
    return unit * gain


def norm_back(value, gain, upstream):
    unit, inverse = statistics(value)
    scaled = upstream * gain
    back = inverse * (
        scaled
        - jnp.mean(scaled, axis=-1, keepdims=True)
        - unit * jnp.mean(scaled * unit, axis=-1, keepdims=True)
    )
    return back, jnp.sum(upstream * unit, axis=0, keepdims=True)


def gelu_parts(value):
    share = 0.5 * (1.0 + lax.erf(value * (0.5**0.5)))
    slope = share + value * jnp.exp(-0.5 * value * value) * 0.3989422804014327
    return value * share, slope


def mm(left, right):
    return lax.dot_general(left, right, (((1,), (0,)), ((), ())), preferred_element_type=F32)


def mm_nt(left, right):
    return lax.dot_general(left, right, (((1,), (1,)), ((), ())), preferred_element_type=F32)


def swap(value, axis, size, mask):
    return lax.ppermute(value, axis, [(i, i ^ mask) for i in range(size)])


def bits_of(size):
    return [1 << b for b in range(size.bit_length() - 1)]


def exchange(value, axis):
    return lax.all_to_all(value, axis, split_axis=0, concat_axis=0, tiled=True)


ANY = pl.BlockSpec(memory_space=pl.ANY)
VMEM = pl.BlockSpec(memory_space=pltpu.VMEM)
SMEM = pl.BlockSpec(memory_space=pltpu.SMEM)


def call(body, outs, *args, specs=None, scratch=(), flops=0, moved=0):
    inner = body.func if isinstance(body, functools.partial) else body
    cost = pl.CostEstimate(flops=int(flops), bytes_accessed=int(moved), transcendentals=0)
    return pl.pallas_call(
        body,
        out_shape=[jax.ShapeDtypeStruct(shape, kind) for shape, kind in outs],
        in_specs=[VMEM] * len(args) if specs is None else specs,
        out_specs=[VMEM] * len(outs),
        scratch_shapes=list(scratch),
        compiler_params=pltpu.CompilerParams(vmem_limit_bytes=VMEM_LIMIT),
        cost_estimate=cost if flops else None,
        name=inner.__name__,
    )(*args)


def shard_copies(me_ref, tp, own, parts, store, sems):
    copies = [own]
    for k in range(1, tp):
        group = []
        if len(parts) == 1:
            source = parts[0].at[me_ref[1] ^ k]
            group.append(pltpu.make_async_copy(source, store.at[k], sems.at[k, 0]))
        else:
            for core, part in enumerate(parts):
                rows = part.shape[1] // 4
                for chip in range(4):
                    source = part.at[k - 1, pl.ds(chip * rows, rows)]
                    target = store.at[k, me_ref[0] ^ (2 * chip + core)]
                    sem = sems.at[k, 2 * chip + core]
                    group.append(pltpu.make_async_copy(source, target, sem))
        copies.append(group)
    for group in copies:
        for copy in group:
            copy.start()

    def wait(k):
        for copy in copies[k]:
            copy.wait()

    return wait


def fetch(me_ref, tp, shard, parts, store, sems):
    own = [pltpu.make_async_copy(shard, store.at[0], sems.at[0, 0])]
    return shard_copies(me_ref, tp, own, parts, store, sems)


def relative_rows(me_ref, order, turned, store, count=None):
    if order is None:
        return turned
    store[...] = turned
    rows = turned.shape[0] >> len(order)
    picked = []
    for m in range(1 << len(order) if count is None else count):
        mask = sum(((m >> (len(order) - 1 - i)) & 1) << bit for i, bit in enumerate(order))
        start = pl.multiple_of((me_ref[0] ^ mask) * rows, rows)
        picked.append(store[pl.ds(start, rows), :])
    return jnp.concatenate(picked, axis=0)


def project(dims, me_ref, blocks, gain, weight, normed, pieces):
    slots, ranks, few, tp, heads = dims
    features = heads * HEAD
    part = slots * few
    pieces[heads * ranks :] = jnp.zeros_like(pieces[heads * ranks :])
    for k in range(tp):
        z = me_ref[1] ^ k
        value = blocks[z].astype(F32).reshape(slots, ranks, few, -1)
        value = jnp.concatenate(
            [value[c, r] for r in range(ranks) for c in range(slots)], axis=0
        )
        low = layer_norm(value, gain[...]).astype(BF)
        normed[z] = low
        columns = pl.ds(pl.multiple_of(z * part, part), part)
        proj = mm_nt(weight[...], low).astype(BF)
        for c in range(heads):
            for r in range(ranks):
                for t in range(3):
                    rows = t * features + c * HEAD
                    piece = proj[rows : rows + HEAD, r * part : (r + 1) * part]
                    pieces[c * ranks + r, t, :, columns] = piece


def tied_softmax(own, other, key_ok, scale):
    depth = own.shape[0] * own.shape[2]
    turned = own[:, 0].reshape(depth, -1).T
    logits = jnp.concatenate(
        [mm(turned, pair[:, 1].reshape(depth, -1)) for pair in (own, other)], axis=1
    )
    ok = key_ok[...] > 0
    masked = jnp.where(ok, logits * scale, NEGATIVE)
    powers = jnp.exp(masked - jnp.max(masked, axis=-1, keepdims=True))
    return masked, powers * (1.0 / jnp.sum(powers, axis=-1, keepdims=True)), ok


def attend(scale, own, other, key_ok, mixed):
    _, probs, _ = tied_softmax(own, other, key_ok, scale)
    depth = own.shape[0] * own.shape[2]
    low = probs.astype(BF)
    half = low.shape[1] // 2
    total = mm_nt(low[:, :half], own[:, 2].reshape(depth, -1))
    total += mm_nt(low[:, half:], other[:, 2].reshape(depth, -1))
    mixed[...] = total.astype(BF).reshape(mixed.shape)


def attend_back(scale, own, other, key_ok, weight, mixed_grad, query_grad, kept, given):
    masked, probs, ok = tied_softmax(own, other, key_ok, scale)
    seqs = own.shape[0]
    depth = seqs * own.shape[2]
    low = probs.astype(BF)
    half = low.shape[1] // 2
    out_grad = mixed_grad[...].reshape(-1, depth)
    prob_grad = jnp.concatenate(
        [mm(out_grad, pair[:, 2].reshape(depth, -1)) for pair in (own, other)], axis=1
    )
    prob_dot = jnp.sum(probs * prob_grad, axis=-1, keepdims=True)
    mean_logit = jnp.sum(jnp.where(ok, probs * masked, 0.0), axis=-1, keepdims=True)
    entropy = jnp.where(ok, probs * (masked - mean_logit), 0.0)
    grad = (probs * (prob_grad - prob_dot) - weight[...] * entropy).astype(BF)
    total = mm_nt(own[:, 1].reshape(depth, -1), grad[:, :half])
    total += mm_nt(other[:, 1].reshape(depth, -1), grad[:, half:])
    query_grad[...] = (total * scale).astype(BF).reshape(query_grad.shape)
    turned = out_grad.T
    flat = own[:, 0].reshape(depth, -1)
    shape = (seqs, HEAD, half)
    given[:, 0] = (mm(flat, grad[:, half:]) * scale).astype(BF).reshape(shape)
    given[:, 1] = mm(turned, low[:, half:]).astype(BF).reshape(shape)
    kept[:, 0] = (mm(flat, grad[:, :half]) * scale).reshape(shape)
    kept[:, 1] = mm(turned, low[:, :half]).reshape(shape)


def column_probs(query, key, rule, scale):
    scores = jnp.where(rule, mm_nt(query, key) * scale, NEGATIVE)
    powers = jnp.exp(scores - jnp.max(scores, axis=-1, keepdims=True))
    return powers * (1.0 / jnp.sum(powers, axis=-1, keepdims=True))


def same_column(count, few):
    rows = lax.broadcasted_iota(jnp.int32, (count, count), 0)
    columns = lax.broadcasted_iota(jnp.int32, (count, count), 1)
    return (rows % few) == (columns % few)


def narrow(store, k, features):
    whole = store[k].reshape(-1, store.shape[3])
    return [whole[i * features : (i + 1) * features] for i in range(5)]


def columns_forward(dims, parts, me_ref, both, arrived, gain, shard, *refs):
    few, tp, heads = dims
    parts, refs = refs[:parts], refs[parts:]
    after_row, normed, proj, right, after_col, store, sems = refs
    wait = fetch(me_ref, tp, shard, parts, store, sems)
    features = heads * HEAD
    seqs = both.shape[0]
    count = seqs * few
    total = both[:, 0].reshape(count, -1).astype(F32)
    attended = []
    for k in range(tp):
        z = me_ref[1] ^ k
        if len(arrived.shape) == 4:
            lanes = []
            for c in range(heads):
                value = arrived[z, c]
                pieces = [value[:, s * HEAD : (s + 1) * HEAD] for s in range(seqs)]
                lanes.append(jnp.concatenate(pieces, axis=0))
            attended.append(jnp.concatenate(lanes, axis=1))
        else:
            attended.append(arrived[z])
        right[k, :, 4 * features : 5 * features] = attended[k]
        right[k, :, 5 * features :] = jnp.zeros_like(right[k, :, 5 * features :])
    update = jnp.zeros_like(total)
    for k in range(tp):
        wait(k)
        update += mm(attended[k], narrow(store, k, features)[0])
    total = total + update
    after_row[...] = total
    low = layer_norm(total, gain[...]).astype(BF)
    normed[...] = low
    rule = same_column(count, few)
    update = jnp.zeros_like(total)
    for k in range(tp):
        weights = narrow(store, k, features)
        for t in range(3):
            proj[t, k] = mm_nt(low, weights[2 + t]).astype(BF)
        mixed = []
        for h in range(heads):
            at = slice(h * HEAD, (h + 1) * HEAD)
            probs = column_probs(proj[0, k, :, at], proj[1, k, :, at], rule, HEAD**-0.5)
            mixed.append(mm(probs.astype(BF), proj[2, k, :, at]).astype(BF))
        mixed = jnp.concatenate(mixed, axis=1)
        right[k, :, 3 * features : 4 * features] = mixed
        update += mm(mixed, weights[1])
    after_col[...] = total + update


def columns_backward(dims, parts, me_ref, *refs):
    few, tp, heads = dims
    middle, outputs, after_row, normed, proj, right, gain, shard = refs[:8]
    parts, refs = refs[8 : 8 + parts], refs[8 + parts :]
    home, left, right_out, row_mixed, gain_grad, store, sems = refs
    wait = fetch(me_ref, tp, shard, parts, store, sems)
    features = heads * HEAD
    count = middle.shape[0]
    seqs = count // few
    middle_low = middle[...].astype(BF)
    left[0] = normed[...]
    left[1] = middle_low
    rule = same_column(count, few)
    upstream = jnp.zeros(middle.shape, F32)
    for k in range(tp):
        wait(k)
        weights = narrow(store, k, features)
        mixed_grad = mm_nt(middle_low, weights[1]).astype(BF)
        grads = [[], [], []]
        for h in range(heads):
            at = slice(h * HEAD, (h + 1) * HEAD)
            query, key, value = proj[0, k, :, at], proj[1, k, :, at], proj[2, k, :, at]
            probs = column_probs(query, key, rule, HEAD**-0.5)
            out_grad = mixed_grad[:, at]
            prob_grad = mm_nt(out_grad, value)
            score = probs * (prob_grad - jnp.sum(probs * prob_grad, axis=-1, keepdims=True))
            score = score.astype(BF)
            grads[0].append((mm(score, key) * HEAD**-0.5).astype(BF))
            grads[1].append((mm(score.T, query) * HEAD**-0.5).astype(BF))
            grads[2].append(mm(probs.astype(BF).T, out_grad).astype(BF))
        for t in range(3):
            grad = jnp.concatenate(grads[t], axis=1)
            upstream += mm(grad, weights[2 + t])
            right_out[k, :, t * features : (t + 1) * features] = grad
        right_out[k, :, 3 * features :] = right[k, :, 3 * features :]
    back, gain_grad[...] = norm_back(after_row[...], gain[...], upstream)
    low = (middle[...] + back).astype(BF)
    home[:, 0] = outputs[...].reshape(seqs, few, -1)
    home[:, 1] = low.reshape(seqs, few, -1)
    left[2] = low
    for k in range(tp):
        z = me_ref[1] ^ k
        value = mm_nt(low, narrow(store, k, features)[0]).astype(BF)
        if len(row_mixed.shape) == 4:
            for c in range(heads):
                lane = value[:, c * HEAD : (c + 1) * HEAD]
                pieces = [lane[s * few : (s + 1) * few] for s in range(seqs)]
                row_mixed[z, c] = jnp.concatenate(pieces, axis=1)
            row_mixed[z, heads:] = jnp.zeros_like(row_mixed[z, heads:])
        else:
            row_mixed[z] = value


def store_halves(halves, z, value):
    rows = value.shape[0] // 2
    for half, part in zip(halves, (value[:rows], value[rows:])):
        half[:, z] = part.reshape(half.shape[0], half.shape[2], -1)


def column_weights(orders, me_ref, left, left_other, right, right_other, *refs):
    tp = right.shape[0]
    qkv, col_out, row_out, rows = refs[0:2], refs[2:4], refs[4:6], refs[6]
    features = col_out[0].shape[3]
    turned = []
    for i in range(3):
        value = jnp.concatenate([left[i], left_other[i]], axis=0).T
        turned.append(relative_rows(me_ref, orders[i], value, rows.at[i], 4))
    for k in range(tp):
        value = jnp.concatenate([right[k], right_other[k]], axis=0)
        start = 0
        for i, (halves, size) in enumerate(((qkv, 3), (col_out, 1), (row_out, 1))):
            columns = slice(start, start + size * features)
            store_halves(halves, me_ref[1] ^ k, mm(turned[i], value[:, columns]).astype(BF))
            start += size * features


def wide_weights(orders, me_ref, left, left_other, right, right_other, *refs):
    rows = refs[4]
    for i, grads in enumerate((refs[0:2], refs[2:4])):
        value = jnp.concatenate([left[i], left_other[i]], axis=0).T
        turned = relative_rows(me_ref, orders[i], value, rows.at[i], 4)
        for k in range(right.shape[1]):
            both = jnp.concatenate([right[i, k], right_other[i, k]], axis=0)
            store_halves(grads, me_ref[1] ^ k, mm(turned, both).astype(BF))


def feed_forward(tp, parts, me_ref, after_col, arrived, gain, up_shard, down_shard, *refs):
    parts, refs = refs[:parts], refs[parts:]
    outputs, middle, gain_grad, left, right, store, sems = refs
    half = store.shape[1] // 2
    own = [
        pltpu.make_async_copy(up_shard, store.at[0, pl.ds(0, half)], sems.at[0, 0]),
        pltpu.make_async_copy(down_shard, store.at[0, pl.ds(half, half)], sems.at[0, 1]),
    ]
    wait = shard_copies(me_ref, tp, own, parts, store, sems)
    value = after_col[...]
    low = layer_norm(value, gain[...]).astype(BF)
    given = arrived[:, 1].reshape(value.shape)
    left[0] = low
    left[1] = given
    result = value
    upstream = jnp.zeros_like(value)
    for k in range(tp):
        wait(k)
        up = store[k, :half].reshape(-1, store.shape[3])
        down = store[k, half:].reshape(-1, store.shape[3])
        hidden, slope = gelu_parts(mm(low, up))
        hidden = hidden.astype(BF)
        right[1, k] = hidden
        result += mm(hidden, down)
        pre_grad = (mm_nt(given, down) * slope).astype(BF)
        right[0, k] = pre_grad
        upstream += mm_nt(pre_grad, up)
    outputs[...] = result.astype(BF)
    back, gain_grad[...] = norm_back(value, gain[...], upstream)
    middle[...] = given.astype(F32) + back


def gather_grads(dims, order, me_ref, back, normed, gain, weight, *outs):
    slots, ranks, few, tp, heads = dims
    features = heads * HEAD
    part = slots * few
    pieces, kept, sent, gain_grad, rows = outs
    total = jnp.zeros((3 * features, normed.shape[2]), F32)
    for k in range(tp):
        z = me_ref[1] ^ k
        columns = pl.ds(pl.multiple_of(z * part, part), part)
        for c in range(heads):
            for r in range(ranks):
                for t in range(3):
                    piece = back[c * ranks + r, t, :, columns]
                    at = t * features + c * HEAD
                    pieces[z, at : at + HEAD, r * part : (r + 1) * part] = piece
        total += mm(pieces[z], normed[z])
    gain_grad[...] = (
        jnp.sum(total * weight[...].astype(F32), axis=0, keepdims=True) / gain[...]
    )
    turned = relative_rows(me_ref, order, total.T.astype(BF), rows)
    half = turned.shape[0] // 2
    kept[...] = turned[:half].reshape(kept.shape)
    sent[...] = turned[half:].reshape(sent.shape)


def finish(dims, parts, me_ref, *refs):
    slots, ranks, few, tp, heads = dims
    features = heads * HEAD
    pieces, tokens, gain, home, shard = refs[:5]
    parts, (result, store, sems) = refs[5 : 5 + parts], refs[5 + parts :]
    wait = fetch(me_ref, tp, shard, parts, store, sems)
    inner = home[:, 1].reshape(tokens.shape)
    upstream = jnp.zeros(inner.shape, F32)
    for k in range(tp):
        wait(k)
        whole = store[k].reshape(-1, store.shape[3])[: 3 * features]
        upstream += mm(pieces[me_ref[1] ^ k].T, whole)
    upstream = upstream.reshape(ranks, slots, few, -1)
    upstream = jnp.concatenate(
        [upstream[r, c] for c in range(slots) for r in range(ranks)], axis=0
    )
    back, _ = norm_back(tokens[...].astype(F32), gain[...], upstream)
    result[...] = (inner.astype(F32) + back).astype(BF)


def after(value, *others):
    return lax.optimization_barrier((value,) + others)[0]


def add(left, right):
    return (left.astype(F32) + right.astype(F32)).astype(BF)


def local(
    tokens,
    cotangent,
    lengths,
    column_mask,
    row_gain,
    row_qkv,
    row_out,
    col_gain,
    col_qkv,
    col_out,
    ffn_gain,
    ffn_up,
    ffn_down,
):
    slots, ranks, tp = lax.axis_size("c"), lax.axis_size("r"), lax.axis_size("tp")
    seqs = slots * ranks
    block, width = tokens.shape[2], tokens.shape[3]
    cols = column_mask.shape[1]
    few = block // seqs
    part = slots * few
    features = row_qkv.shape[2]
    heads = features // HEAD
    hidden = ffn_up.shape[1]
    queries = tp * part
    count = seqs * few
    tied_scale = (HEAD * seqs) ** (-0.5)
    my_seq, my_rank, my_z = lax.axis_index(SEQ), lax.axis_index("r"), lax.axis_index("tp")
    me_ref = jnp.stack([my_seq, my_z]).astype(jnp.int32)
    dims = (slots, ranks, few, tp, heads)
    fast = seqs == 8 and ranks == 2
    row_gain, col_gain, ffn_gain = row_gain[None], col_gain[None], ffn_gain[None]

    penalty_scale = ENTROPY_WEIGHT * (seqs * cols) / (HEADS * jnp.sum(lengths).astype(F32))
    position = jnp.arange(cols, dtype=jnp.int32).reshape(tp, slots, ranks, few)
    position = position.transpose(2, 0, 1, 3)
    flag = column_mask.reshape(tp, slots, ranks, few).transpose(2, 0, 1, 3)
    valid = (position < lengths[0]) & ((flag == 1) | (position == 0))
    valid = valid.astype(F32).reshape(ranks, queries)
    key_ok = jnp.concatenate(
        [lax.dynamic_index_in_dim(valid, my_rank ^ k, 0) for k in range(ranks)], axis=1
    )
    query_position = lax.dynamic_index_in_dim(position.reshape(ranks, queries), my_rank, 0)
    query_weight = jnp.where(query_position < lengths[0], penalty_scale, 0.0).reshape(queries, 1)

    own = tokens[0, 0]
    both = [value.reshape(seqs, few, width) for value in (own, cotangent[0, 0])]
    both = exchange(jnp.stack(both, axis=1), SEQ)

    row_weight = row_qkv.transpose(0, 2, 1).reshape(3 * features, width)
    shard_a = jnp.concatenate(
        [row_out, col_out, col_qkv.transpose(0, 2, 1).reshape(3 * features, width)]
    )

    def cut(shard, least):
        rows = shard.shape[0]
        rows += -rows % (seqs * least)
        shard = jnp.pad(shard, ((0, rows - shard.shape[0]), (0, 0)))
        return shard.reshape(seqs, rows // seqs, width)

    shard_a = cut(shard_a, 16 if fast else 1)
    shard_c = cut(row_weight, 16 if fast else 1)
    shard_b = cut(jnp.concatenate([ffn_up, ffn_down]), 1)

    def mine(shard):
        return lax.dynamic_index_in_dim(shard, my_seq, 0, keepdims=False)

    def everyone(value):
        return exchange(jnp.broadcast_to(value, (tp,) + value.shape), "tp")

    def along_tp(piece):
        return jnp.stack([swap(piece, "tp", tp, k) for k in range(1, tp)])

    def along_plane(held):
        return [swap(held, "c", slots, mask) for mask in (1, 2)]

    def across_plane(near):
        half = near[0].shape[1] // 2
        one = swap(near[0][:, :half], "c", slots, 2)
        return [one, swap(near[1][:, half:], "c", slots, 1)]

    def along_cores(parts):
        held = jnp.concatenate(parts, axis=1)
        return [held, swap(held, "r", ranks, 1)]

    if fast:
        near_a = along_tp(mine(shard_a))
        blocks = everyone(after(own, near_a, both))
        plane_a = along_plane(near_a)
        cross_a = across_plane(plane_a)
        parts_a = along_cores([near_a] + plane_a + cross_a)
        near_b = along_tp(after(mine(shard_b), blocks))
        blocks = after(blocks, *cross_a)
    else:
        blocks = everyone(own)

        def everywhere(shard):
            rows = shard.shape[0] * shard.shape[1]
            whole = lax.all_gather(mine(shard), ("tp",) + SEQ, axis=0)
            return [whole.reshape(tp, 8, rows // 8, width)]

        parts_a, parts_b, parts_c = everywhere(shard_a), everywhere(shard_b), everywhere(shard_c)
        shard_a = shard_a.reshape(8, -1, width)
        shard_c = shard_c.reshape(8, -1, width)
    up_own = ffn_up.reshape(4, -1, width)
    down_own = ffn_down.reshape(4, -1, width)
    store_a = pltpu.VMEM((tp,) + shard_a.shape, BF)
    store_b = pltpu.VMEM((tp, 8, shard_b.shape[0] * shard_b.shape[1] // 8, width), BF)
    store_c = pltpu.VMEM((tp,) + shard_c.shape, BF)
    sems = pltpu.SemaphoreType.DMA((tp, 10))

    if fast:
        normed, pieces = call(
            functools.partial(project, dims),
            [((tp, block, width), BF), ((seqs, 3, HEAD, queries), BF)],
            me_ref,
            blocks,
            row_gain,
            row_weight,
            specs=[SMEM] + [VMEM] * 3,
            flops=2 * cols * width * 3 * features,
            moved=8 << 20,
        )
    else:
        order = blocks.reshape(tp, slots, ranks, few, width).transpose(0, 2, 1, 3, 4)
        normed = layer_norm(order.astype(F32), row_gain).astype(BF).reshape(tp, block, width)
        pieces = jnp.einsum("fd,zld->fzl", row_weight, normed, preferred_element_type=F32)
        pieces = pieces.astype(BF).reshape(3, heads, HEAD, tp, ranks, part)
        pieces = pieces.transpose(1, 4, 0, 2, 3, 5).reshape(heads, ranks, 3, HEAD, queries)
        pieces = jnp.pad(pieces, ((0, slots - heads),) + ((0, 0),) * 4)
        pieces = pieces.reshape(seqs, 3, HEAD, queries)
    pieces = exchange(pieces, SEQ)
    mixed_shape = (tp * slots, few, seqs * HEAD)
    if fast:
        pieces, near_b, *parts_a = lax.optimization_barrier((pieces, near_b, *parts_a))
        others = swap(pieces, "r", ranks, 1)
        plane_b = along_plane(near_b)
        (mixed,) = call(
            functools.partial(attend, tied_scale),
            [(mixed_shape, BF)],
            pieces,
            others,
            key_ok,
            flops=4 * cols * queries * seqs * HEAD,
            moved=8 << 20,
        )
    else:
        pairs = lax.all_gather(pieces[:, 1:], "r", axis=0)
        pairs = pairs.transpose(2, 1, 3, 0, 4).reshape(2, seqs * HEAD, cols)
        key, value = pairs[0], pairs[1]
        query = pieces[:, 0].reshape(seqs * HEAD, queries)
        key_ok = valid.reshape(1, cols)
        logits = jnp.einsum("ki,kj->ij", query, key, preferred_element_type=F32) * tied_scale
        masked = jnp.where(key_ok > 0, logits, NEGATIVE)
        powers = jnp.exp(masked - jnp.max(masked, axis=-1, keepdims=True))
        probs = powers / jnp.sum(powers, axis=-1, keepdims=True)
        mixed = jnp.einsum("ij,kj->ik", probs.astype(BF), value, preferred_element_type=F32)
        mixed = mixed.astype(BF).reshape(mixed_shape)
    mixed = exchange(mixed, ("tp", "c"))
    shards = (tp, count, features)
    if fast:
        arrived = after(mixed, *plane_b).reshape(tp, slots, few, seqs * HEAD)
        parts_b = along_cores([near_b] + plane_b + across_plane(plane_b))
        near_c = along_tp(after(mine(shard_c), mixed))
    else:
        arrived = (
            mixed.reshape(tp, slots, few, seqs, HEAD)[:, :heads]
            .transpose(0, 3, 2, 1, 4)
            .reshape(shards)
        )

    flat = (count, width)
    packed = (tp, count, 5 * features + -5 * features % 128)
    n_parts = len(parts_a)
    after_row, col_normed, col_proj, col_right, after_col = call(
        functools.partial(columns_forward, (few, tp, heads), n_parts),
        [(flat, F32), (flat, BF), ((3,) + shards, BF), (packed, BF), (flat, F32)],
        me_ref,
        both,
        arrived,
        col_gain,
        shard_a,
        *parts_a,
        specs=[SMEM] + [VMEM] * 3 + [ANY] * (1 + n_parts),
        scratch=[store_a, sems],
        flops=2 * count * width * width * 5,
        moved=20 << 20,
    )
    if fast:
        after_col = after(after_col, near_c)
    outputs, middle, ffn_gain_grad, wide_left, wide_right = call(
        functools.partial(feed_forward, tp, n_parts),
        [
            (flat, BF),
            (flat, F32),
            ((1, width), F32),
            ((2,) + flat, BF),
            ((2, tp, count, hidden), BF),
        ],
        me_ref,
        after_col,
        both,
        ffn_gain,
        up_own,
        down_own,
        *parts_b,
        specs=[SMEM] + [VMEM] * 3 + [ANY] * (2 + n_parts),
        scratch=[store_b, sems],
        flops=2 * count * width * hidden * tp * 4,
        moved=30 << 20,
    )
    home, col_left, col_right, row_mixed, col_gain_grad = call(
        functools.partial(columns_backward, (few, tp, heads), n_parts),
        [
            ((seqs, 2, few, width), BF),
            ((3,) + flat, BF),
            (packed, BF),
            ((tp, slots, few, seqs * HEAD) if fast else shards, BF),
            ((1, width), F32),
        ],
        me_ref,
        middle,
        outputs,
        after_row,
        col_normed,
        col_proj,
        col_right,
        col_gain,
        shard_a,
        *parts_a,
        specs=[SMEM] + [VMEM] * 7 + [ANY] * (1 + n_parts),
        scratch=[store_a, sems],
        flops=2 * count * width * width * 8,
        moved=30 << 20,
    )

    def halve(kept, came):
        half = kept.shape[0] // 2
        return add(kept[:half], came[:half]), add(kept[half:], came[half:])

    def give(sent, mask):
        return swap(sent, "c", slots, mask)

    def last(held):
        return jnp.sum(exchange(held, "tp").astype(F32), axis=0)

    def all_at_once(left, right):
        grad = jnp.einsum("ld,zlf->zdf", left, right, preferred_element_type=F32).astype(BF)
        grad = lax.psum_scatter(grad, SEQ, scatter_dimension=1, tiled=True)
        return lax.psum_scatter(grad, "tp", scatter_dimension=0, tiled=True)[0].astype(F32)

    rows_of = width // seqs
    turned_rows = pltpu.VMEM((3, width, 2 * count), BF)
    if fast:
        wide_others = swap(wide_left, "r", ranks, 1), swap(wide_right, "r", ranks, 1)
        col_others = swap(col_left, "r", ranks, 1), swap(col_right, "r", ranks, 1)
        up_kept, up_sent, down_kept, down_sent = call(
            functools.partial(wide_weights, ((0, 2, 1), (0, 1, 2))),
            [((2, tp, rows_of, hidden), BF)] * 4,
            me_ref,
            wide_left,
            wide_others[0],
            wide_right,
            wide_others[1],
            specs=[SMEM] + [VMEM] * 4,
            scratch=[turned_rows],
            flops=2 * count * width * hidden * tp * 2,
            moved=30 << 20,
        )
        qkv_kept, qkv_sent, *outs_halves = call(
            functools.partial(column_weights, ((0, 2, 1), (0, 1, 2), (0, 1, 2))),
            [((2, tp, rows_of, 3 * features), BF)] * 2
            + [((2, tp, rows_of, features), BF)] * 4,
            me_ref,
            after(col_left, up_sent),
            col_others[0],
            col_right,
            col_others[1],
            specs=[SMEM] + [VMEM] * 4,
            scratch=[turned_rows],
            flops=2 * count * width * width * 5,
            moved=12 << 20,
        )
    else:
        row_mixed = row_mixed.reshape(tp, seqs, few, heads, HEAD).transpose(0, 3, 2, 1, 4)
        row_mixed = jnp.pad(row_mixed, ((0, 0), (0, slots - heads)) + ((0, 0),) * 3)
        my_order = my_z ^ jnp.arange(tp)
        col_right = col_right[my_order]
    row_mixed = exchange(row_mixed.reshape(mixed_shape), ("tp", "c"))
    if fast:
        up_came, down_came = give(up_sent, 2), give(down_sent, 1)
        row_mixed = after(row_mixed, qkv_sent)
        query_grad, kept, sent = call(
            functools.partial(attend_back, tied_scale),
            [
                ((seqs, HEAD, queries), BF),
                ((seqs, 2, HEAD, queries), F32),
                ((seqs, 2, HEAD, queries), BF),
            ],
            pieces,
            others,
            key_ok,
            query_weight,
            row_mixed,
            flops=10 * cols * queries * seqs * HEAD,
            moved=16 << 20,
        )
        sent = after(sent, up_came, down_came)
        pair_grad = (kept + swap(sent, "r", ranks, 1).astype(F32)).astype(BF)
        back = jnp.concatenate([query_grad[:, None], pair_grad], axis=1)
    else:
        out_grad = row_mixed.reshape(queries, seqs * HEAD)
        prob_grad = jnp.einsum("ik,kj->ij", out_grad, value, preferred_element_type=F32)
        prob_dot = jnp.sum(probs * prob_grad, axis=-1, keepdims=True)
        mean_logit = jnp.sum(
            jnp.where(key_ok > 0, probs * masked, 0.0), axis=-1, keepdims=True
        )
        entropy = jnp.where(key_ok > 0, probs * (masked - mean_logit), 0.0)
        grad = (probs * (prob_grad - prob_dot) - query_weight * entropy).astype(BF)
        total = jnp.einsum("ij,kj->ki", grad, key, preferred_element_type=F32)
        query_grad = (total * tied_scale).astype(BF).reshape(seqs, HEAD, queries)
        key_grad = jnp.einsum("ki,ij->kj", query, grad, preferred_element_type=F32)
        value_grad = jnp.einsum(
            "ik,ij->kj", out_grad, probs.astype(BF), preferred_element_type=F32
        )
        both = jnp.stack([(key_grad * tied_scale).astype(BF), value_grad.astype(BF)])
        both = both.reshape(2, seqs, HEAD, ranks, queries).transpose(3, 1, 0, 2, 4)
        pair_grad = lax.psum_scatter(both, "r", scatter_dimension=0, tiled=False)
        back = jnp.concatenate([query_grad[:, None], pair_grad], axis=1)
    back = exchange(back, SEQ)
    if fast:
        home = after(home, back)
    home = exchange(home, SEQ)
    outputs = home[:, 0].reshape(block, width)
    if fast:
        (up_kept, up_sent), (down_kept, down_sent) = halve(up_kept, up_came), halve(down_kept, down_came)
        up_came, down_came = give(up_sent, 1), give(down_sent, 2)
        wide_last = jnp.concatenate(
            [add(up_kept, up_came)[0], add(down_kept, down_came)[0]], axis=-1
        )
        col_out_kept, col_out_sent, row_out_kept, row_out_sent = outs_halves
        outs_kept = jnp.concatenate([col_out_kept, row_out_kept], axis=3)
        outs_sent = jnp.concatenate([col_out_sent, row_out_sent], axis=3)
        near_c, qkv_sent, outs_sent, back = lax.optimization_barrier(
            (near_c, qkv_sent, outs_sent, after(back, up_came, down_came))
        )
        qkv_came, outs_came = give(qkv_sent, 2), give(outs_sent, 1)
        plane_c = along_plane(near_c)
        parts_c = along_cores([near_c] + plane_c + across_plane(plane_c))
        traded, kept, sent, row_gain_grad = call(
            functools.partial(gather_grads, dims, (0, 2, 1)),
            [((tp, 3 * features, block), BF)]
            + [((4, rows_of, 3 * features), BF)] * 2
            + [((1, width), F32)],
            me_ref,
            back,
            normed,
            row_gain,
            row_weight,
            specs=[SMEM] + [VMEM] * 4,
            scratch=[pltpu.VMEM((width, 3 * features), BF)],
            flops=2 * cols * width * 3 * features,
            moved=8 << 20,
        )
    else:
        both = back.reshape(slots, ranks, 3, HEAD, tp, part)[:heads]
        both = both.transpose(4, 2, 0, 3, 1, 5).reshape(tp, 3 * features, block)
        row_grad = jnp.einsum("zld,zfl->df", normed, both, preferred_element_type=F32)
        row_gain_grad = (
            jnp.sum(row_grad.T * row_weight.astype(F32), axis=0, keepdims=True) / row_gain
        )
        traded = both
    traded = exchange(traded, "tp")
    if fast:
        row_gain_grad = after(row_gain_grad, traded)
    gains = jnp.concatenate([row_gain_grad, col_gain_grad, ffn_gain_grad], axis=0)
    for axis, size in (("r", ranks), ("c", slots), ("tp", tp)):
        for k in bits_of(size):
            gains = gains + swap(gains, axis, size, k)
    if fast:
        came = swap(sent, "r", ranks, 1)
        kept, sent = add(kept[:2], came[:2]), add(kept[2:], came[2:])
        kept, sent = halve(kept, give(sent, 2))
        row_grad = add(kept[0], give(sent, 1)[0]).astype(F32)
        (qkv_kept, qkv_sent), (outs_kept, outs_sent) = halve(qkv_kept, qkv_came), halve(outs_kept, outs_came)
        small = jnp.concatenate(
            [add(qkv_kept, give(qkv_sent, 1))[0], add(outs_kept, give(outs_sent, 2))[0]], axis=-1
        )
        wide_grad = last(after(wide_last, traded))
        small = last(small)
        qkv, outs = small[:, : 3 * features], small[:, 3 * features :]
        up_grad, down_grad = wide_grad[:, :hidden], wide_grad[:, hidden:]
    (input_grad,) = call(
        functools.partial(finish, dims, n_parts),
        [((block, width), BF)],
        me_ref,
        traded,
        own,
        row_gain,
        home,
        shard_c,
        *parts_c,
        specs=[SMEM] + [VMEM] * 4 + [ANY] * (1 + n_parts),
        scratch=[store_c, sems],
        flops=2 * block * width * width * 3,
        moved=8 << 20,
    )
    if not fast:
        row_grad = lax.psum_scatter(row_grad, SEQ, scatter_dimension=0, tiled=True)
        wide_right = wide_right[:, my_order]
        up_grad = all_at_once(wide_left[0], wide_right[0])
        down_grad = all_at_once(wide_left[1], wide_right[1])
        qkv = all_at_once(col_left[0], col_right[..., : 3 * features])
        outs = jnp.concatenate(
            [
                all_at_once(col_left[1], col_right[..., 3 * features : 4 * features]),
                all_at_once(col_left[2], col_right[..., 4 * features : 5 * features]),
            ],
            axis=1,
        )

    def thirds(value):
        return value.reshape(width // seqs, 3, features).transpose(1, 0, 2)

    return (
        outputs[None, None],
        input_grad[None, None],
        gains[0],
        thirds(row_grad),
        outs[:, features:].T,
        gains[1],
        thirds(qkv),
        outs[:, :features].T,
        gains[2],
        up_grad,
        down_grad.T,
    )


def solution(mesh):
    seqs, tp = mesh.shape["seq"], mesh.shape["tp"]
    heads = HEADS // tp
    slots = 1 << (heads - 1).bit_length()
    split = Mesh(mesh.devices.reshape(slots, seqs // slots, tp), ("c", "r", "tp"))
    return jax.shard_map(
        local,
        mesh=split,
        in_specs=(
            P(None, SEQ, "tp", None),
            P(None, SEQ, "tp", None),
            P(),
            P(),
            P(),
            P(None, None, "tp"),
            P("tp", None),
            P(),
            P(None, None, "tp"),
            P("tp", None),
            P(),
            P(None, "tp"),
            P("tp", None),
        ),
        out_specs=(
            P(None, SEQ, "tp", None),
            P(None, SEQ, "tp", None),
            P(),
            P(None, SEQ, "tp"),
            P("tp", SEQ),
            P(),
            P(None, SEQ, "tp"),
            P("tp", SEQ),
            P(),
            P(SEQ, "tp"),
            P("tp", SEQ),
        ),
        check_vma=False,
    )
```

profile of v0, /device:TPU:0, one launch (start us, length us, event | category | flops | bytes accessed | tf_op | source)
XLA Modules:
  0.0 428.0 jit_solution(17024614223914313645)
XLA Ops:
  2.8 5.2 %all-to-all-start = ((bf16[8,2,32,768]{3,2,1,0:T(8,128)(2,1)}), bf16[8,2,32,768]{3,2,1,0:T(8,128)(2,1)S(1)}, u32[]{:S(2)}, u32[]{:S(2)}) async-start(bf16[8,2,32,768]{3,2,1,0:T(8,128)(2,1)} %pad_maximum_fusion.4), calls=%async_computation | async-start | bytes 1572864 | tf_op jit(solution)/shard_map/all_to_all | solution.py:69
  13.4 13.0 %collective-permute-done.1 = bf16[128,768]{1,0:T(8,128)(2,1)S(1)} collective-permute-done((bf16[128,768]{1,0:T(8,128)(2,1)S(1)}, bf16[128,768]{1,0:T(8,128)(2,1)S(1)}, u32[]{:S(2)}, u32[]{:S(2)}) %collective-permute-start.1) | collective-permute-done | bytes 196640 | tf_op jit(solution)/shard_map/ppermute | solution.py:61
  29.6 6.7 %all-to-all-start.1 = ((bf16[4,256,768]{2,1,0:T(8,128)(2,1)}), bf16[4,256,768]{2,1,0:T(8,128)(2,1)}, u32[]{:S(2)}, u32[]{:S(2)}) async-start(bf16[4,256,768]{2,1,0:T(8,128)(2,1)} %broadcast_in_dim.26), calls=%async_computation.1 | async-start | bytes 3145728 | tf_op jit(solution)/shard_map/all_to_all | solution.py:69
  39.4 11.9 %collective-permute-done.3 = bf16[3,128,768]{2,1,0:T(8,128)(2,1)S(1)} collective-permute-done((bf16[3,128,768]{2,1,0:T(8,128)(2,1)S(1)}, bf16[3,128,768]{2,1,0:T(8,128)(2,1)S(1)}, u32[]{:S(2)}, u32[]{:S(2)}) %collective-permute-start.3) | collective-permute-done | bytes 589856 | tf_op jit(solution)/shard_map/ppermute | solution.py:61
  62.7 11.6 %all-to-all-done.1.blocks = bf16[4,256,768]{2,1,0:T(8,128)(2,1)} async-done(((bf16[4,256,768]{2,1,0:T(8,128)(2,1)}), bf16[4,256,768]{2,1,0:T(8,128)(2,1)}, u32[]{:S(2)}, u32[]{:S(2)}) %all-to-all-start.1) | async-done | bytes 1572896 | tf_op jit(solution)/shard_map/all_to_all | solution.py:69
  89.5 9.3 %collective-permute-done.7 = bf16[192,768]{1,0:T(8,128)(2,1)S(1)} collective-permute-done((bf16[192,768]{1,0:T(8,128)(2,1)S(1)}, bf16[192,768]{1,0:T(8,128)(2,1)S(1)}, u32[]{:S(2)}, u32[]{:S(2)}) %collective-permute-start.7) | collective-permute-done | bytes 294944 | tf_op jit(solution)/shard_map/ppermute | solution.py:61
  98.8 9.8 %collective-permute-done.8 = bf16[192,768]{1,0:T(8,128)(2,1)S(1)} collective-permute-done((bf16[192,768]{1,0:T(8,128)(2,1)S(1)}, bf16[192,768]{1,0:T(8,128)(2,1)S(1)}, u32[]{:S(2)}, u32[]{:S(2)}) %collective-permute-start.8) | collective-permute-done | bytes 294944 | tf_op jit(solution)/shard_map/ppermute | solution.py:61
  112.2 17.1 %collective-permute-done.12 = bf16[3,192,768]{2,1,0:T(8,128)(2,1)S(1)} collective-permute-done((bf16[3,192,768]{2,1,0:T(8,128)(2,1)S(1)}, bf16[3,192,768]{2,1,0:T(8,128)(2,1)S(1)}, u32[]{:S(2)}, u32[]{:S(2)}) %collective-permute-start.12) | collective-permute-done | bytes 884768 | tf_op jit(solution)/shard_map/ppermute | solution.py:61
  143.5 6.6 %collective-permute-done.11.other = bf16[8,3,64,512]{3,2,1,0:T(8,128)(2,1)S(1)} collective-permute-done((bf16[8,3,64,512]{3,2,1,0:T(8,128)(2,1)}, bf16[8,3,64,512]{3,2,1,0:T(8,128)(2,1)S(1)}, u32[]{:S(2)}, u32[]{:S(2)}) %collective-permute-start.11) | collective-permute-done | bytes 1572896 | tf_op jit(solution)/shard_map/ppermute | solution.py:61
  155.9 10.4 %all-to-all-start.3 = ((bf16[16,32,512]{2,1,0:T(8,128)(2,1)}), bf16[16,32,512]{2,1,0:T(8,128)(2,1)S(1)}, u32[]{:S(2)}, u32[]{:S(2)}) async-start(bf16[16,32,512]{2,1,0:T(8,128)(2,1)} %attend.1), calls=%async_computation.3 | async-start | bytes 1048576 | tf_op jit(solution)/shard_map/all_to_all | solution.py:69
  167.6 13.8 %all-to-all-done.3 = bf16[16,32,512]{2,1,0:T(8,128)(2,1)S(1)} async-done(((bf16[16,32,512]{2,1,0:T(8,128)(2,1)}), bf16[16,32,512]{2,1,0:T(8,128)(2,1)S(1)}, u32[]{:S(2)}, u32[]{:S(2)}) %all-to-all-start.3) | async-done | bytes 524320 | tf_op jit(solution)/shard_map/all_to_all | solution.py:69
  185.8 12.6 %columns_forward.1 = (f32[256,768]{1,0:T(8,128)}, bf16[256,768]{1,0:T(8,128)(2,1)}, bf16[3,4,256,192]{3,2,1,0:T(8,128)(2,1)}, bf16[4,256,1024]{2,1,0:T(8,128)(2,1)}, f32[256,768]{1,0:T(8,128)}) custom-call(s32[2]{0:T(128)} %pad_add_fusion.me_ref, bf16[8,2,32,768]{3,2,1,0:T(8,128)(2,1)} %copy-done.8, bf16[4,4,32,512]{3,2,1,0:T(8,128)(2,1)} %bitcast.80, ...), custom_call_target="tpu_custom_call" | custom-call | flops 1509949440 | bytes 20971520 | tf_op jit(solution)/shard_map/columns_forward/pallas_call | solution.py:80
  199.2 11.1 %feed_forward.1 = (bf16[256,768]{1,0:T(8,128)(2,1)}, f32[256,768]{1,0:T(8,128)}, f32[1,768]{1,0:T(1,128)}, bf16[2,256,768]{2,1,0:T(8,128)(2,1)}, bf16[2,4,256,768]{3,2,1,0:T(8,128)(2,1)}) custom-call(s32[2]{0:T(128)} %pad_add_fusion.me_ref, f32[256,768]{1,0:T(8,128)} %get-tuple-element.77.after_col, bf16[8,2,32,768]{3,2,1,0:T(8,128)(2,1)} %copy-done.8, ...), custom_call_target="tpu_custom_call" | custom-call | flops 4831838208 | bytes 31457280 | tf_op jit(solution)/shard_map/feed_forward/pallas_call | solution.py:80
  210.4 17.1 %columns_backward.1 = (bf16[8,2,32,768]{3,2,1,0:T(8,128)(2,1)}, bf16[3,256,768]{2,1,0:T(8,128)(2,1)}, bf16[4,256,1024]{2,1,0:T(8,128)(2,1)}, bf16[4,4,32,512]{3,2,1,0:T(8,128)(2,1)}, f32[1,768]{1,0:T(1,128)}) custom-call(s32[2]{0:T(128)} %pad_add_fusion.me_ref, f32[256,768]{1,0:T(8,128)} %get-tuple-element.78.refs_0_, ...), custom_call_target="tpu_custom_call" | custom-call | flops 2415919104 | bytes 31457280 | tf_op jit(solution)/shard_map/columns_backward/pallas_call | solution.py:80
  233.3 8.2 %wide_weights.1 = (bf16[2,4,96,768]{3,2,1,0:T(8,128)(2,1)}, bf16[2,4,96,768]{3,2,1,0:T(8,128)(2,1)}, bf16[2,4,96,768]{3,2,1,0:T(8,128)(2,1)}, bf16[2,4,96,768]{3,2,1,0:T(8,128)(2,1)}) custom-call(s32[2]{0:T(128)} %pad_add_fusion.me_ref, bf16[2,256,768]{2,1,0:T(8,128)(2,1)} %get-tuple-element.87.left, ...), custom_call_target="tpu_custom_call" | custom-call | flops 2415919104 | bytes 31457280 | tf_op jit(solution)/shard_map/wide_weights/pallas_call | solution.py:80
  247.0 7.1 %column_weights.1 = (bf16[2,4,96,576]{3,2,1,0:T(8,128)(2,1)}, bf16[2,4,96,576]{3,2,1,0:T(8,128)(2,1)}, bf16[2,4,96,192]{3,2,1,0:T(8,128)(2,1)}, bf16[2,4,96,192]...) custom-call(s32[2]{0:T(128)} %pad_add_fusion.me_ref, ...), custom_call_target="tpu_custom_call" | custom-call | flops 1509949440 | bytes 12582912 | tf_op jit(solution)/shard_map/column_weights/pallas_call | solution.py:80
  254.2 7.5 %attend_back.1 = (bf16[8,64,512]{2,1,0:T(8,128)(2,1)}, f32[8,2,64,512]{3,2,1,0:T(8,128)}, bf16[8,2,64,512]{3,2,1,0:T(8,128)(2,1)}) custom-call(bf16[8,3,64,512]{3,2,1,0:T(8,128)(2,1)} %all-to-all-done.2.own, bf16[8,3,64,512]{3,2,1,0:T(8,128)(2,1)} %copy-done.33, f32[1,1024]{1,0:T(1,128)} %pad_maximum_fusion.11.key_ok, f32[512,1]{1,0:T(8,128)} %copy.40.weight, ...), custom_call_target="tpu_custom_call" | custom-call | flops 2684354560 | bytes 16777216 | tf_op jit(solution)/shard_map/attend_back/pallas_call | solution.py:80
  261.7 9.5 %collective-permute-done.24 = bf16[2,4,96,768]{3,2,1,0:T(8,128)(2,1)} collective-permute-done((bf16[2,4,96,768]{3,2,1,0:T(8,128)(2,1)}, bf16[2,4,96,768]{3,2,1,0:T(8,128)(2,1)}, u32[]{:S(2)}, u32[]{:S(2)}) %collective-permute-start.24) | collective-permute-done | bytes 1179680 | tf_op jit(solution)/shard_map/ppermute | solution.py:61
  288.1 14.8 %all-to-all-done.5.back = bf16[8,3,64,512]{3,2,1,0:T(8,128)(2,1)S(1)} async-done(((bf16[8,3,64,512]{3,2,1,0:T(8,128)(2,1)}), bf16[8,3,64,512]{3,2,1,0:T(8,128)(2,1)S(1)}, u32[]{:S(2)}, u32[]{:S(2)}) %all-to-all-start.5) | async-done | bytes 1572896 | tf_op jit(solution)/shard_map/all_to_all | solution.py:69
  308.6 6.2 %collective-permute-done.27 = bf16[1,4,96,768]{3,2,1,0:T(8,128)(2,1)} collective-permute-done((bf16[1,4,96,768]{3,2,1,0:T(8,128)(2,1)}, bf16[1,4,96,768]{3,2,1,0:T(8,128)(2,1)}, u32[]{:S(2)}, u32[]{:S(2)}) %collective-permute-start.27) | collective-permute-done | bytes 589856 | tf_op jit(solution)/shard_map/ppermute | solution.py:61
  329.0 6.4 %collective-permute-done.44 = bf16[2,4,96,384]{3,2,1,0:T(8,128)(2,1)} collective-permute-done((bf16[2,4,96,384]{3,2,1,0:T(8,128)(2,1)}, bf16[2,4,96,384]{3,2,1,0:T(8,128)(2,1)}, u32[]{:S(2)}, u32[]{:S(2)}) %collective-permute-start.44) | collective-permute-done | bytes 589856 | tf_op jit(solution)/shard_map/ppermute | solution.py:61
  338.0 6.2 %collective-permute-done.42 = bf16[2,4,96,576]{3,2,1,0:T(8,128)(2,1)} collective-permute-done((bf16[2,4,96,576]{3,2,1,0:T(8,128)(2,1)}, bf16[2,4,96,576]{3,2,1,0:T(8,128)(2,1)}, u32[]{:S(2)}, u32[]{:S(2)}) %collective-permute-start.42) | collective-permute-done | bytes 884768 | tf_op jit(solution)/shard_map/ppermute | solution.py:61
  351.0 8.7 %collective-permute-done.43 = bf16[1,4,96,576]{3,2,1,0:T(8,128)(2,1)S(1)} collective-permute-done((bf16[1,4,96,576]{3,2,1,0:T(8,128)(2,1)S(1)}, bf16[1,4,96,576]{3,2,1,0:T(8,128)(2,1)S(1)}, u32[]{:S(2)}, u32[]{:S(2)}) %collective-permute-start.43) | collective-permute-done | bytes 442400 | tf_op jit(solution)/shard_map/ppermute | solution.py:61
  417.5 6.5 %finish.1 = bf16[256,768]{1,0:T(8,128)(2,1)} custom-call(s32[2]{0:T(128)} %pad_add_fusion.me_ref, bf16[4,576,256]{2,1,0:T(8,128)(2,1)} %copy-done.4, bf16[256,768]{1,0:T(8,128)(2,1)} %bitcast.77, f32[1,768]{1,0:T(1,128)} %broadcast_in_dim.27.gain.refs_2_, bf16[8,2,32,768]{3,2,1,0:T(8,128)(2,1)} %copy-done.3, bf16[8,80,768]{2,1,0:T(8,128)(2,1)} %bitcast.72, ...), custom_call_target="tpu_custom_call" | custom-call | flops 905969664 | bytes 8388608 | tf_op jit(solution)/shard_map/finish/pallas_call | solution.py:80
  (253 shorter events, 188.4 us)
Async XLA Ops:
  2.8 25.4 %all-to-all-start = ((bf16[8,2,32,768]{3,2,1,0:T(8,128)(2,1)}), bf16[8,2,32,768]{3,2,1,0:T(8,128)(2,1)S(1)}, u32[]{:S(2)}, u32[]{:S(2)}) async-start(bf16[8,2,32,768]{3,2,1,0:T(8,128)(2,1)} %pad_maximum_fusion.4), calls=%async_computation | async-start | bytes 1572864 | tf_op jit(solution)/shard_map/all_to_all | solution.py:69
  29.6 44.7 %all-to-all-start.1 = ((bf16[4,256,768]{2,1,0:T(8,128)(2,1)}), bf16[4,256,768]{2,1,0:T(8,128)(2,1)}, u32[]{:S(2)}, u32[]{:S(2)}) async-start(bf16[4,256,768]{2,1,0:T(8,128)(2,1)} %broadcast_in_dim.26), calls=%async_computation.1 | async-start | bytes 3145728 | tf_op jit(solution)/shard_map/all_to_all | solution.py:69
  61.5 47.2 %collective-permute-start.10 = (bf16[3,512,768]{2,1,0:T(8,128)(2,1)}, bf16[3,512,768]{2,1,0:T(8,128)(2,1)S(1)}, u32[]{:S(2)}, u32[]{:S(2)}) collective-permute-start(bf16[3,512,768]{2,1,0:T(8,128)(2,1)} %constant_dynamic-update-slice_fusion.refs_0_.refs_8_), channel_id=1, source_target_pairs={{0,4},{4,0},{1,5},{5,1},{2,6},{6,2},{3,7},{7,3},{8,12},{12,8},{9,1... | collective-permute-start | bytes 7077896 | tf_op jit(solution)/shard_map/ppermute | solution.py:61
  79.1 29.6 %all-to-all-start.2 = ((bf16[8,3,64,512]{3,2,1,0:T(8,128)(2,1)}), bf16[8,3,64,512]{3,2,1,0:T(8,128)(2,1)}, u32[]{:S(2)}, u32[]{:S(2)}) async-start(bf16[8,3,64,512]{3,2,1,0:T(8,128)(2,1)} %get-tuple-element.68), calls=%async_computation.2 | async-start | bytes 3145728 | tf_op jit(solution)/shard_map/all_to_all | solution.py:69
  85.1 23.5 %collective-permute-start.8 = (bf16[192,768]{1,0:T(8,128)(2,1)S(1)}, bf16[192,768]{1,0:T(8,128)(2,1)S(1)}, u32[]{:S(2)}, u32[]{:S(2)}) collective-permute-start(bf16[192,768]{1,0:T(8,128)(2,1)S(1)} %dynamic-slice_bitcast_fusion), channel_id=1, source_target_pairs={{0,2},{1,3},{2,0},{3,1},{4,6},{5,7},{6,4},{7,5},{8,10},{9,11},{10,... | collective-permute-start | bytes 884744 | tf_op jit(solution)/shard_map/ppermute | solution.py:61
  86.4 22.2 %collective-permute-start.9 = (bf16[192,768]{1,0:T(8,128)(2,1)S(1)}, bf16[192,768]{1,0:T(8,128)(2,1)S(1)}, u32[]{:S(2)}, u32[]{:S(2)}) collective-permute-start(bf16[192,768]{1,0:T(8,128)(2,1)S(1)} %dynamic-slice_bitcast_fusion), channel_id=1, source_target_pairs={{0,3},{1,2},{2,1},{3,0},{4,7},{5,6},{6,5},{7,4},{8,11},{9,10},{10,... | collective-permute-start | bytes 884744 | tf_op jit(solution)/shard_map/ppermute | solution.py:61
  108.8 20.5 %collective-permute-start.12 = (bf16[3,192,768]{2,1,0:T(8,128)(2,1)S(1)}, bf16[3,192,768]{2,1,0:T(8,128)(2,1)S(1)}, u32[]{:S(2)}, u32[]{:S(2)}) collective-permute-start(bf16[3,192,768]{2,1,0:T(8,128)(2,1)S(1)} %pad_maximum_fusion.3), channel_id=1, source_target_pairs={{0,8},{8,0},{16,24},{24,16},{1,9},{9,1},{17,25},{25,17},{2,10},{10... | collective-permute-start | bytes 2654216 | tf_op jit(solution)/shard_map/ppermute | solution.py:61
  141.5 57.7 %collective-permute-start.19 = (bf16[3,768,768]{2,1,0:T(8,128)(2,1)}, bf16[3,768,768]{2,1,0:T(8,128)(2,1)}, u32[]{:S(2)}, u32[]{:S(2)}) collective-permute-start(bf16[3,768,768]{2,1,0:T(8,128)(2,1)} %constant_dynamic-update-slice_fusion.5.refs_0_), channel_id=1, source_target_pairs={{0,4},{4,0},{1,5},{5,1},{2,6},{6,2},{3,7},{7,3},{8,12},{12,8},{9,1... | collective-permute-start | bytes 10616840 | tf_op jit(solution)/shard_map/ppermute | solution.py:61
  155.9 25.5 %all-to-all-start.3 = ((bf16[16,32,512]{2,1,0:T(8,128)(2,1)}), bf16[16,32,512]{2,1,0:T(8,128)(2,1)S(1)}, u32[]{:S(2)}, u32[]{:S(2)}) async-start(bf16[16,32,512]{2,1,0:T(8,128)(2,1)} %attend.1), calls=%async_computation.3 | async-start | bytes 1048576 | tf_op jit(solution)/shard_map/all_to_all | solution.py:69
  210.3 23.0 %collective-permute-start.21 = (bf16[2,4,256,768]{3,2,1,0:T(8,128)(2,1)}, bf16[2,4,256,768]{3,2,1,0:T(8,128)(2,1)}, u32[]{:S(2)}, u32[]{:S(2)}) collective-permute-start(bf16[2,4,256,768]{3,2,1,0:T(8,128)(2,1)} %get-tuple-element.88.right), channel_id=1, source_target_pairs={{0,4},{4,0},{1,5},{5,1},{2,6},{6,2},{3,7},{7,3},{8,12},{12,8},{9,1... | collective-permute-start | bytes 9437192 | tf_op jit(solution)/shard_map/ppermute | solution.py:61
  228.5 25.6 %all-to-all-start.4 = ((bf16[16,32,512]{2,1,0:T(8,128)(2,1)}), bf16[16,32,512]{2,1,0:T(8,128)(2,1)}, u32[]{:S(2)}, u32[]{:S(2)}) async-start(bf16[16,32,512]{2,1,0:T(8,128)(2,1)} %bitcast.86), calls=%async_computation.4 | async-start | bytes 1048576 | tf_op jit(solution)/shard_map/all_to_all | solution.py:69
  241.5 29.7 %collective-permute-start.24 = (bf16[2,4,96,768]{3,2,1,0:T(8,128)(2,1)}, bf16[2,4,96,768]{3,2,1,0:T(8,128)(2,1)}, u32[]{:S(2)}, u32[]{:S(2)}) collective-permute-start(bf16[2,4,96,768]{3,2,1,0:T(8,128)(2,1)} %get-tuple-element.89), channel_id=1, source_target_pairs={{0,16},{8,24},{16,0},{24,8},{1,17},{9,25},{17,1},{25,9},{2,18},{10... | collective-permute-start | bytes 3538952 | tf_op jit(solution)/shard_map/ppermute | solution.py:61
  243.1 28.6 %collective-permute-start.25 = (bf16[2,4,96,768]{3,2,1,0:T(8,128)(2,1)}, bf16[2,4,96,768]{3,2,1,0:T(8,128)(2,1)S(1)}, u32[]{:S(2)}, u32[]{:S(2)}) collective-permute-start(bf16[2,4,96,768]{3,2,1,0:T(8,128)(2,1)} %get-tuple-element.97), channel_id=1, source_target_pairs={{0,8},{8,0},{16,24},{24,16},{1,9},{9,1},{17,25},{25,17},{2,10},{10... | collective-permute-start | bytes 3538952 | tf_op jit(solution)/shard_map/ppermute | solution.py:61
  277.8 25.1 %all-to-all-start.5 = ((bf16[8,3,64,512]{3,2,1,0:T(8,128)(2,1)}), bf16[8,3,64,512]{3,2,1,0:T(8,128)(2,1)S(1)}, u32[]{:S(2)}, u32[]{:S(2)}) async-start(bf16[8,3,64,512]{3,2,1,0:T(8,128)(2,1)} %pad_maximum_fusion.1), calls=%async_computation.5 | async-start | bytes 3145728 | tf_op jit(solution)/shard_map/all_to_all | solution.py:69
  283.7 31.1 %collective-permute-start.27 = (bf16[1,4,96,768]{3,2,1,0:T(8,128)(2,1)}, bf16[1,4,96,768]{3,2,1,0:T(8,128)(2,1)}, u32[]{:S(2)}, u32[]{:S(2)}) collective-permute-start(bf16[1,4,96,768]{3,2,1,0:T(8,128)(2,1)} %add_convert_fusion.6), channel_id=1, source_target_pairs={{0,8},{8,0},{16,24},{24,16},{1,9},{9,1},{17,25},{25,17},{2,10},{10... | collective-permute-start | bytes 1769480 | tf_op jit(solution)/shard_map/ppermute | solution.py:61
  286.6 28.1 %collective-permute-start.28 = (bf16[1,4,96,768]{3,2,1,0:T(8,128)(2,1)}, bf16[1,4,96,768]{3,2,1,0:T(8,128)(2,1)S(1)}, u32[]{:S(2)}, u32[]{:S(2)}) collective-permute-start(bf16[1,4,96,768]{3,2,1,0:T(8,128)(2,1)} %add_convert_fusion.5), channel_id=1, source_target_pairs={{0,16},{8,24},{16,0},{24,8},{1,17},{9,25},{17,1},{25,9},{2,18},{10... | collective-permute-start | bytes 1769480 | tf_op jit(solution)/shard_map/ppermute | solution.py:61
  303.0 21.2 %all-to-all-start.6 = ((bf16[8,2,32,768]{3,2,1,0:T(8,128)(2,1)}), bf16[8,2,32,768]{3,2,1,0:T(8,128)(2,1)S(1)}, u32[]{:S(2)}, u32[]{:S(2)}) async-start(bf16[8,2,32,768]{3,2,1,0:T(8,128)(2,1)} %get-tuple-element.99), calls=%async_computation.6 | async-start | bytes 1572864 | tf_op jit(solution)/shard_map/all_to_all | solution.py:69
  314.8 29.4 %collective-permute-start.42 = (bf16[2,4,96,576]{3,2,1,0:T(8,128)(2,1)}, bf16[2,4,96,576]{3,2,1,0:T(8,128)(2,1)}, u32[]{:S(2)}, u32[]{:S(2)}) collective-permute-start(bf16[2,4,96,576]{3,2,1,0:T(8,128)(2,1)} %get-tuple-element.116), channel_id=1, source_target_pairs={{0,16},{8,24},{16,0},{24,8},{1,17},{9,25},{17,1},{25,9},{2,18},{10... | collective-permute-start | bytes 2654216 | tf_op jit(solution)/shard_map/ppermute | solution.py:61
  324.1 37.9 %all-to-all-start.7 = ((bf16[4,576,256]{2,1,0:T(8,128)(2,1)}), bf16[4,576,256]{2,1,0:T(8,128)(2,1)S(1)}, u32[]{:S(2)}, u32[]{:S(2)}) async-start(bf16[4,576,256]{2,1,0:T(8,128)(2,1)} %get-tuple-element.107), calls=%async_computation.7 | async-start | bytes 2359296 | tf_op jit(solution)/shard_map/all_to_all | solution.py:69
  348.0 22.1 %collective-permute-start.29 = (bf16[3,80,768]{2,1,0:T(8,128)(2,1)}, bf16[3,80,768]{2,1,0:T(8,128)(2,1)}, u32[]{:S(2)}, u32[]{:S(2)}) collective-permute-start(bf16[3,80,768]{2,1,0:T(8,128)(2,1)} %pad_maximum_fusion.8), channel_id=1, source_target_pairs={{0,8},{8,0},{16,24},{24,16},{1,9},{9,1},{17,25},{25,17},{2,10},{10... | collective-permute-start | bytes 1105928 | tf_op jit(solution)/shard_map/ppermute | solution.py:61
  349.1 22.0 %collective-permute-start.30 = (bf16[3,80,768]{2,1,0:T(8,128)(2,1)}, bf16[3,80,768]{2,1,0:T(8,128)(2,1)}, u32[]{:S(2)}, u32[]{:S(2)}) collective-permute-start(bf16[3,80,768]{2,1,0:T(8,128)(2,1)} %pad_maximum_fusion.8), channel_id=1, source_target_pairs={{0,16},{8,24},{16,0},{24,8},{1,17},{9,25},{17,1},{25,9},{2,18},{10... | collective-permute-start | bytes 1105928 | tf_op jit(solution)/shard_map/ppermute | solution.py:61
  362.0 21.6 %all-to-all-start.8 = ((bf16[4,96,960]{2,1,0:T(8,128)(2,1)}), bf16[4,96,960]{2,1,0:T(8,128)(2,1)S(1)}, u32[]{:S(2)}, u32[]{:S(2)}) async-start(bf16[4,96,960]{2,1,0:T(8,128)(2,1)} %pad_maximum_fusion.5), calls=%async_computation.8 | async-start | bytes 1572864 | tf_op jit(solution)/shard_map/all_to_all | solution.py:69
  379.8 37.6 %collective-permute-start.33 = (bf16[3,320,768]{2,1,0:T(8,128)(2,1)}, bf16[3,320,768]{2,1,0:T(8,128)(2,1)}, u32[]{:S(2)}, u32[]{:S(2)}) collective-permute-start(bf16[3,320,768]{2,1,0:T(8,128)(2,1)} %constant_dynamic-update-slice_fusion.10.refs_5_), channel_id=1, source_target_pairs={{0,4},{4,0},{1,5},{5,1},{2,6},{6,2},{3,7},{7,3},{8,12},{12,8},{9,1... | collective-permute-start | bytes 4423688 | tf_op jit(solution)/shard_map/ppermute | solution.py:61
  384.5 42.3 %all-to-all-start.9 = ((bf16[4,96,1536]{2,1,0:T(8,128)(2,1)}), bf16[4,96,1536]{2,1,0:T(8,128)(2,1)S(1)}, u32[]{:S(2)}, u32[]{:S(2)}) async-start(bf16[4,96,1536]{2,1,0:T(8,128)(2,1)} %pad_maximum_fusion.2), calls=%async_computation.9 | async-start | bytes 2359296 | tf_op jit(solution)/shard_map/all_to_all | solution.py:69
  (67 other events, 788.7 us)
where the time goes:
time: 435 us; the launch traced here: 428 us
  waiting for transfers between devices  179 us (41%)
  starting transfers between devices  105 us (24%)
  Pallas kernels  83.9 us (19%)
  local copies, waits for them, and re-layouts  30.4 us (7%)
  other arithmetic  27 us (6%)
    ppermute x46, waiting for transfers between devices, swap(): return lax.ppermute(value, axis, [(i, i ^ mask) for i in range(size)])  134 us
    pallas_call x10, Pallas kernels, call(): pl.pallas_call(body, out_shape=[jax.ShapeDtypeStruct(shape, kind) for sha...  83.9 us
    ppermute x46, starting transfers between devices, swap(): return lax.ppermute(value, axis, [(i, i ^ mask) for i in range(size)])  54 us
    all_to_all x10, starting transfers between devices, exchange(): return lax.all_to_all(value, axis, split_axis=0, concat_axis=0, tiled=True)  51.3 us
    all_to_all x10, waiting for transfers between devices, exchange(): return lax.all_to_all(value, axis, split_axis=0, concat_axis=0, tiled=True)  44.9 us
    unnamed x85, local copies, waits for them, and re-layouts  19 us
  transfers between devices with their start and end apart: 56, of which 30 were waited for; matrix products, arithmetic and copies ran while one was open for 11% of the time, Pallas kernels for 17%

commit v1 on v0

--- a/solution.py
+++ b/solution.py
@@ -76,7 +76,7 @@
 
 def call(body, outs, *args, specs=None, scratch=(), flops=0, moved=0):
     inner = body.func if isinstance(body, functools.partial) else body
-    cost = pl.CostEstimate(flops=int(flops), bytes_accessed=int(moved), transcendentals=0)
+    cost = pl.CostEstimate(flops=int(flops), bytes_accessed=2 * int(moved), transcendentals=0)
     return pl.pallas_call(
         body,
         out_shape=[jax.ShapeDtypeStruct(shape, kind) for shape, kind in outs],
@@ -134,14 +134,15 @@
     return jnp.concatenate(picked, axis=0)
 
 
-def project(dims, me_ref, blocks, gain, weight, normed, pieces):
+def project(dims, me_ref, *refs):
     slots, ranks, few, tp, heads = dims
+    blocks, (gain, weight, normed, pieces) = refs[:tp], refs[tp:]
     features = heads * HEAD
     part = slots * few
     pieces[heads * ranks :] = jnp.zeros_like(pieces[heads * ranks :])
     for k in range(tp):
         z = me_ref[1] ^ k
-        value = blocks[z].astype(F32).reshape(slots, ranks, few, -1)
+        value = blocks[k][...].astype(F32).reshape(slots, ranks, few, -1)
         value = jnp.concatenate(
             [value[c, r] for r in range(ranks) for c in range(slots)], axis=0
         )
@@ -419,7 +420,7 @@
     pieces, tokens, gain, home, shard = refs[:5]
     parts, (result, store, sems) = refs[5 : 5 + parts], refs[5 + parts :]
     wait = fetch(me_ref, tp, shard, parts, store, sems)
-    inner = home[:, 1].reshape(tokens.shape)
+    inner = home[:, few : 2 * few].reshape(tokens.shape)
     upstream = jnp.zeros(inner.shape, F32)
     for k in range(tp):
         wait(k)
@@ -435,6 +436,20 @@
 
 def after(value, *others):
     return lax.optimization_barrier((value,) + others)[0]
+
+
+def together(*values):
+    return lax.optimization_barrier(values)
+
+
+def two_terms(gains):
+    high = lax.reduce_precision(gains, 8, 7)
+    low = gains - high
+    return jnp.pad(jnp.concatenate([high, low], axis=0), ((0, 10), (0, 0))).astype(BF)
+
+
+def one_term(rows):
+    return rows[:3] + rows[3:6]
 
 
 def add(left, right):
@@ -488,7 +503,7 @@
 
     own = tokens[0, 0]
     both = [value.reshape(seqs, few, width) for value in (own, cotangent[0, 0])]
-    both = exchange(jnp.stack(both, axis=1), SEQ)
+    both = jnp.stack(both, axis=1)
 
     row_weight = row_qkv.transpose(0, 2, 1).reshape(3 * features, width)
     shard_a = jnp.concatenate(
@@ -508,9 +523,6 @@
     def mine(shard):
         return lax.dynamic_index_in_dim(shard, my_seq, 0, keepdims=False)
 
-    def everyone(value):
-        return exchange(jnp.broadcast_to(value, (tp,) + value.shape), "tp")
-
     def along_tp(piece):
         return jnp.stack([swap(piece, "tp", tp, k) for k in range(1, tp)])
 
@@ -526,16 +538,20 @@
         held = jnp.concatenate(parts, axis=1)
         return [held, swap(held, "r", ranks, 1)]
 
+    def blocks_of(value):
+        return [own] + [swap(value, "tp", tp, k) for k in range(1, tp)]
+
     if fast:
         near_a = along_tp(mine(shard_a))
-        blocks = everyone(after(own, near_a, both))
+        sent, both, near_a = together(own, both, near_a)
+        blocks = blocks_of(sent)
+        both = exchange(both, SEQ)
         plane_a = along_plane(near_a)
-        cross_a = across_plane(plane_a)
-        parts_a = along_cores([near_a] + plane_a + cross_a)
-        near_b = along_tp(after(mine(shard_b), blocks))
-        blocks = after(blocks, *cross_a)
+        blocks[1], blocks[2], blocks[3], both, *plane_a = together(*blocks[1:], both, *plane_a)
+        near_b = along_tp(after(mine(shard_b), blocks[1]))
     else:
-        blocks = everyone(own)
+        blocks = blocks_of(own)
+        both = exchange(both, SEQ)
 
         def everywhere(shard):
             rows = shard.shape[0] * shard.shape[1]
@@ -557,27 +573,33 @@
             functools.partial(project, dims),
             [((tp, block, width), BF), ((seqs, 3, HEAD, queries), BF)],
             me_ref,
-            blocks,
+            *blocks,
             row_gain,
             row_weight,
-            specs=[SMEM] + [VMEM] * 3,
+            specs=[SMEM] + [VMEM] * (tp + 2),
             flops=2 * cols * width * 3 * features,
             moved=8 << 20,
         )
     else:
-        order = blocks.reshape(tp, slots, ranks, few, width).transpose(0, 2, 1, 3, 4)
+        order = jnp.stack(blocks)[my_z ^ jnp.arange(tp)]
+        order = order.reshape(tp, slots, ranks, few, width).transpose(0, 2, 1, 3, 4)
         normed = layer_norm(order.astype(F32), row_gain).astype(BF).reshape(tp, block, width)
         pieces = jnp.einsum("fd,zld->fzl", row_weight, normed, preferred_element_type=F32)
         pieces = pieces.astype(BF).reshape(3, heads, HEAD, tp, ranks, part)
         pieces = pieces.transpose(1, 4, 0, 2, 3, 5).reshape(heads, ranks, 3, HEAD, queries)
         pieces = jnp.pad(pieces, ((0, slots - heads),) + ((0, 0),) * 4)
         pieces = pieces.reshape(seqs, 3, HEAD, queries)
+    if fast:
+        pieces, *plane_a = together(pieces, *plane_a)
+        cross_a = across_plane(plane_a)
     pieces = exchange(pieces, SEQ)
     mixed_shape = (tp * slots, few, seqs * HEAD)
     if fast:
-        pieces, near_b, *parts_a = lax.optimization_barrier((pieces, near_b, *parts_a))
+        pieces, near_b, *cross_a = together(pieces, near_b, *cross_a)
         others = swap(pieces, "r", ranks, 1)
+        others, near_b = together(others, near_b)
         plane_b = along_plane(near_b)
+        parts_a = along_cores([near_a] + plane_a + cross_a)
         (mixed,) = call(
             functools.partial(attend, tied_scale),
             [(mixed_shape, BF)],
@@ -599,11 +621,15 @@
         probs = powers / jnp.sum(powers, axis=-1, keepdims=True)
         mixed = jnp.einsum("ij,kj->ik", probs.astype(BF), value, preferred_element_type=F32)
         mixed = mixed.astype(BF).reshape(mixed_shape)
+    if fast:
+        mixed, parts_a[1], *plane_b = together(mixed, parts_a[1], *plane_b)
+        cross_b = across_plane(plane_b)
     mixed = exchange(mixed, ("tp", "c"))
     shards = (tp, count, features)
     if fast:
-        arrived = after(mixed, *plane_b).reshape(tp, slots, few, seqs * HEAD)
-        parts_b = along_cores([near_b] + plane_b + across_plane(plane_b))
+        mixed, *cross_b = together(mixed, *cross_b)
+        arrived = mixed.reshape(tp, slots, few, seqs * HEAD)
+        parts_b = along_cores([near_b] + plane_b + cross_b)
         near_c = along_tp(after(mine(shard_c), mixed))
     else:
         arrived = (
@@ -630,7 +656,8 @@
         moved=20 << 20,
     )
     if fast:
-        after_col = after(after_col, near_c)
+        after_col, near_c = together(after_col, near_c)
+        plane_c = along_plane(near_c)
     outputs, middle, ffn_gain_grad, wide_left, wide_right = call(
         functools.partial(feed_forward, tp, n_parts),
         [
@@ -731,6 +758,7 @@
         col_right = col_right[my_order]
     row_mixed = exchange(row_mixed.reshape(mixed_shape), ("tp", "c"))
     if fast:
+        up_sent, down_sent, *plane_c = together(up_sent, down_sent, *plane_c)
         up_came, down_came = give(up_sent, 2), give(down_sent, 1)
         row_mixed = after(row_mixed, qkv_sent)
         query_grad, kept, sent = call(
@@ -750,7 +778,17 @@
         )
         sent = after(sent, up_came, down_came)
         pair_grad = (kept + swap(sent, "r", ranks, 1).astype(F32)).astype(BF)
+        (up_kept, up_sent), (down_kept, down_sent) = halve(up_kept, up_came), halve(down_kept, down_came)
+        up_came, down_came = give(up_sent, 1), give(down_sent, 2)
         back = jnp.concatenate([query_grad[:, None], pair_grad], axis=1)
+        back, up_came, down_came = together(back, up_came, down_came)
+        wide_last = jnp.concatenate(
+            [add(up_kept, up_came)[0], add(down_kept, down_came)[0]], axis=-1
+        )
+        wide_came = [
+            swap(lax.dynamic_index_in_dim(wide_last, my_z ^ k, keepdims=False), "tp", tp, k)
+            for k in range(1, tp)
+        ]
     else:
         out_grad = row_mixed.reshape(queries, seqs * HEAD)
         prob_grad = jnp.einsum("ik,kj->ij", out_grad, value, preferred_element_type=F32)
@@ -772,23 +810,15 @@
         back = jnp.concatenate([query_grad[:, None], pair_grad], axis=1)
     back = exchange(back, SEQ)
     if fast:
-        home = after(home, back)
-    home = exchange(home, SEQ)
-    outputs = home[:, 0].reshape(block, width)
-    if fast:
-        (up_kept, up_sent), (down_kept, down_sent) = halve(up_kept, up_came), halve(down_kept, down_came)
-        up_came, down_came = give(up_sent, 1), give(down_sent, 2)
-        wide_last = jnp.concatenate(
-            [add(up_kept, up_came)[0], add(down_kept, down_came)[0]], axis=-1
-        )
         col_out_kept, col_out_sent, row_out_kept, row_out_sent = outs_halves
         outs_kept = jnp.concatenate([col_out_kept, row_out_kept], axis=3)
         outs_sent = jnp.concatenate([col_out_sent, row_out_sent], axis=3)
-        near_c, qkv_sent, outs_sent, back = lax.optimization_barrier(
-            (near_c, qkv_sent, outs_sent, after(back, up_came, down_came))
-        )
+        qkv_sent, outs_sent, back, *rest = together(qkv_sent, outs_sent, back, *plane_c, *wide_came)
+        plane_c, wide_came = rest[:2], rest[2:]
         qkv_came, outs_came = give(qkv_sent, 2), give(outs_sent, 1)
-        plane_c = along_plane(near_c)
+        wide_grad = lax.dynamic_index_in_dim(wide_last, my_z, keepdims=False).astype(F32)
+        for value in wide_came:
+            wide_grad = wide_grad + value.astype(F32)
         parts_c = along_cores([near_c] + plane_c + across_plane(plane_c))
         traded, kept, sent, row_gain_grad = call(
             functools.partial(gather_grads, dims, (0, 2, 1)),
@@ -813,26 +843,37 @@
             jnp.sum(row_grad.T * row_weight.astype(F32), axis=0, keepdims=True) / row_gain
         )
         traded = both
-    traded = exchange(traded, "tp")
-    if fast:
-        row_gain_grad = after(row_gain_grad, traded)
     gains = jnp.concatenate([row_gain_grad, col_gain_grad, ffn_gain_grad], axis=0)
-    for axis, size in (("r", ranks), ("c", slots), ("tp", tp)):
-        for k in bits_of(size):
-            gains = gains + swap(gains, axis, size, k)
-    if fast:
+    home = home.reshape(seqs, 2 * few, width)
+    if fast:
+        traded = exchange(traded, "tp")
         came = swap(sent, "r", ranks, 1)
+        home, traded, qkv_came, outs_came, came = together(home, traded, qkv_came, outs_came, came)
+        (qkv_kept, qkv_sent), (outs_kept, outs_sent) = halve(qkv_kept, qkv_came), halve(outs_kept, outs_came)
+        qkv_came, outs_came = give(qkv_sent, 1), give(outs_sent, 2)
+        ends = jnp.broadcast_to(two_terms(gains), (seqs, 16, width))
+        home = exchange(jnp.concatenate([home, ends], axis=1), SEQ)
+        gains = one_term(jnp.sum(home[:, 2 * few :].astype(F32), axis=0))
         kept, sent = add(kept[:2], came[:2]), add(kept[2:], came[2:])
         kept, sent = halve(kept, give(sent, 2))
         row_grad = add(kept[0], give(sent, 1)[0]).astype(F32)
-        (qkv_kept, qkv_sent), (outs_kept, outs_sent) = halve(qkv_kept, qkv_came), halve(outs_kept, outs_came)
         small = jnp.concatenate(
-            [add(qkv_kept, give(qkv_sent, 1))[0], add(outs_kept, give(outs_sent, 2))[0]], axis=-1
-        )
-        wide_grad = last(after(wide_last, traded))
-        small = last(small)
+            [add(qkv_kept, qkv_came)[0], add(outs_kept, outs_came)[0]], axis=-1
+        )
+        ends = jnp.pad(two_terms(gains), ((0, 0), (0, small.shape[2] - width)))
+        ends = jnp.broadcast_to(ends, (tp,) + ends.shape)
+        small = last(jnp.concatenate([small, ends], axis=1))
+        gains = one_term(small[rows_of:, :width])
+        small = small[:rows_of]
         qkv, outs = small[:, : 3 * features], small[:, 3 * features :]
         up_grad, down_grad = wide_grad[:, :hidden], wide_grad[:, hidden:]
+    else:
+        traded = exchange(traded, "tp")
+        home = exchange(home, SEQ)
+        for axis, size in (("r", ranks), ("c", slots), ("tp", tp)):
+            for k in bits_of(size):
+                gains = gains + swap(gains, axis, size, k)
+    outputs = home[:, :few].reshape(block, width)
     (input_grad,) = call(
         functools.partial(finish, dims, n_parts),
         [((block, width), BF)],

time: 435 us -> 425 us (0.977)
  waiting for transfers between devices: 179 us -> 168 us
    all_to_all x10 -> x8, waiting for transfers between devices: 44.9 us -> 6.25 us  [exchange(): return lax.all_to_all(value, axis, split_axis=0, concat_axis=0, tiled=True)]
    ppermute x46 -> x47, waiting for transfers between devices: 134 us -> 162 us  [swap(): return lax.ppermute(value, axis, [(i, i ^ mask) for i in range(size)])]
    ppermute x46 -> x47, starting transfers between devices: 54 us -> 65.4 us  [swap(): return lax.ppermute(value, axis, [(i, i ^ mask) for i in range(size)])]
    all_to_all x10 -> x8, starting transfers between devices: 51.3 us -> 43.6 us  [exchange(): return lax.all_to_all(value, axis, split_axis=0, concat_axis=0, tiled=True)]
    unnamed x85 -> x108, local copies, waits for them, and re-layouts: 19 us -> 18.6 us
  transfers between devices with their start and end apart: 56 -> 55, of which waited for: 30 -> 22; matrix products, arithmetic and copies ran while one was open for 11% -> 10% of each run, Pallas kernels for 17% -> 15%
where the time goes in v1:
time: 425 us; the launch traced here: 419 us
  waiting for transfers between devices  168 us (40%)
  starting transfers between devices  109 us (26%)
  Pallas kernels  84.6 us (20%)
  local copies, waits for them, and re-layouts  30.1 us (7%)
  other arithmetic  24.7 us (6%)
    ppermute x47, waiting for transfers between devices, swap(): return lax.ppermute(value, axis, [(i, i ^ mask) for i in range(size)])  162 us
    pallas_call x10, Pallas kernels, call(): pl.pallas_call(body, out_shape=[jax.ShapeDtypeStruct(shape, kind) for sha...  84.6 us
    ppermute x47, starting transfers between devices, swap(): return lax.ppermute(value, axis, [(i, i ^ mask) for i in range(size)])  65.4 us
    all_to_all x8, starting transfers between devices, exchange(): return lax.all_to_all(value, axis, split_axis=0, concat_axis=0, tiled=True)  43.6 us
    unnamed x108, local copies, waits for them, and re-layouts  18.6 us
  transfers between devices with their start and end apart: 55, of which 22 were waited for; matrix products, arithmetic and copies ran while one was open for 10% of the time, Pallas kernels for 15%

profile of v1, /device:TPU:0, one launch (start us, length us, event | category | flops | bytes accessed | tf_op | source)
XLA Modules:
  0.0 418.9 jit_solution(3750533441052158044)
XLA Ops:
  8.9 11.7 %collective-permute-done.1 = bf16[128,768]{1,0:T(8,128)(2,1)S(1)} collective-permute-done((bf16[128,768]{1,0:T(8,128)(2,1)S(1)}, bf16[128,768]{1,0:T(8,128)(2,1)S(1)}, u32[]{:S(2)}, u32[]{:S(2)}) %collective-permute-start.1) | collective-permute-done | bytes 196640 | tf_op jit(solution)/shard_map/ppermute | solution.py:61
  36.6 12.2 %collective-permute-done.3.refs_1_ = bf16[256,768]{1,0:T(8,128)(2,1)S(1)} collective-permute-done((bf16[256,768]{1,0:T(8,128)(2,1)S(1)}, bf16[256,768]{1,0:T(8,128)(2,1)S(1)}, u32[]{:S(2)}, u32[]{:S(2)}) %collective-permute-start.3) | collective-permute-done | bytes 393248 | tf_op jit(solution)/shard_map/ppermute | solution.py:61
  48.8 13.0 %collective-permute-done.4.refs_2_ = bf16[256,768]{1,0:T(8,128)(2,1)} collective-permute-done((bf16[256,768]{1,0:T(8,128)(2,1)S(1)}, bf16[256,768]{1,0:T(8,128)(2,1)}, u32[]{:S(2)}, u32[]{:S(2)}) %collective-permute-start.4) | collective-permute-done | bytes 393248 | tf_op jit(solution)/shard_map/ppermute | solution.py:61
  71.8 7.4 %collective-permute-start.8 = (bf16[192,768]{1,0:T(8,128)(2,1)S(1)}, bf16[192,768]{1,0:T(8,128)(2,1)S(1)}, u32[]{:S(2)}, u32[]{:S(2)}) collective-permute-start(bf16[192,768]{1,0:T(8,128)(2,1)S(1)} %dynamic-slice_bitcast_fusion), channel_id=1, source_target_pairs={{0,1},{1,0},{2,3},{3,2},{4,5},{5,4},{6,7},{7,6},{8,9},{9,8},{10,11... | collective-permute-start | bytes 884744 | tf_op jit(solution)/shard_map/ppermute | solution.py:61
  86.3 6.7 %collective-permute-done.8 = bf16[192,768]{1,0:T(8,128)(2,1)S(1)} collective-permute-done((bf16[192,768]{1,0:T(8,128)(2,1)S(1)}, bf16[192,768]{1,0:T(8,128)(2,1)S(1)}, u32[]{:S(2)}, u32[]{:S(2)}) %collective-permute-start.8) | collective-permute-done | bytes 294944 | tf_op jit(solution)/shard_map/ppermute | solution.py:61
  93.0 9.7 %collective-permute-done.9 = bf16[192,768]{1,0:T(8,128)(2,1)S(1)} collective-permute-done((bf16[192,768]{1,0:T(8,128)(2,1)S(1)}, bf16[192,768]{1,0:T(8,128)(2,1)S(1)}, u32[]{:S(2)}, u32[]{:S(2)}) %collective-permute-start.9) | collective-permute-done | bytes 294944 | tf_op jit(solution)/shard_map/ppermute | solution.py:61
  117.1 12.5 %collective-permute-done.15 = bf16[3,192,768]{2,1,0:T(8,128)(2,1)} collective-permute-done((bf16[3,192,768]{2,1,0:T(8,128)(2,1)S(1)}, bf16[3,192,768]{2,1,0:T(8,128)(2,1)}, u32[]{:S(2)}, u32[]{:S(2)}) %collective-permute-start.15) | collective-permute-done | bytes 884768 | tf_op jit(solution)/shard_map/ppermute | solution.py:61
  131.1 10.3 %all-to-all-start.2 = ((bf16[16,32,512]{2,1,0:T(8,128)(2,1)}), bf16[16,32,512]{2,1,0:T(8,128)(2,1)S(1)}, u32[]{:S(2)}, u32[]{:S(2)}) async-start(bf16[16,32,512]{2,1,0:T(8,128)(2,1)} %attend.1), calls=%async_computation.2 | async-start | bytes 1048576 | tf_op jit(solution)/shard_map/all_to_all | solution.py:69
  149.6 8.6 %collective-permute-done.17 = bf16[3,96,768]{2,1,0:T(8,128)(2,1)S(1)} collective-permute-done((bf16[3,96,768]{2,1,0:T(8,128)(2,1)S(1)}, bf16[3,96,768]{2,1,0:T(8,128)(2,1)S(1)}, u32[]{:S(2)}, u32[]{:S(2)}) %collective-permute-start.17) | collective-permute-done | bytes 442400 | tf_op jit(solution)/shard_map/ppermute | solution.py:61
  166.8 12.6 %columns_forward.1 = (f32[256,768]{1,0:T(8,128)}, bf16[256,768]{1,0:T(8,128)(2,1)}, bf16[3,4,256,192]{3,2,1,0:T(8,128)(2,1)}, bf16[4,256,1024]{2,1,0:T(8,128)(2,1)}, f32[256,768]{1,0:T(8,128)}) custom-call(s32[2]{0:T(128)} %pad_add_fusion.me_ref, bf16[8,2,32,768]{3,2,1,0:T(8,128)(2,1)} %copy-done.7, bf16[4,4,32,512]{3,2,1,0:T(8,128)(2,1)} %bitcast.89, ...), custom_call_target="tpu_custom_call" | custom-call | flops 1509949440 | bytes 41943040 | tf_op jit(solution)/shard_map/columns_forward/pallas_call | solution.py:80
  179.5 11.1 %feed_forward.1 = (bf16[256,768]{1,0:T(8,128)(2,1)}, f32[256,768]{1,0:T(8,128)}, f32[1,768]{1,0:T(1,128)}, bf16[2,256,768]{2,1,0:T(8,128)(2,1)}, bf16[2,4,256,768]{3,2,1,0:T(8,128)(2,1)}) custom-call(s32[2]{0:T(128)} %pad_add_fusion.me_ref, f32[256,768]{1,0:T(8,128)} %get-tuple-element.124.after_col, bf16[8,2,32,768]{3,2,1,0:T(8,128)(2,1)} %copy-done.7, ...), custom_call_target="tpu_custom_call" | custom-call | flops 4831838208 | bytes 62914560 | tf_op jit(solution)/shard_map/feed_forward/pallas_call | solution.py:80
  190.7 17.1 %columns_backward.1 = (bf16[8,2,32,768]{3,2,1,0:T(8,128)(2,1)}, bf16[3,256,768]{2,1,0:T(8,128)(2,1)}, bf16[4,256,1024]{2,1,0:T(8,128)(2,1)}, bf16[4,4,32,512]{3,2,1,0:T(8,128)(2,1)}, f32[1,768]{1,0:T(1,128)}) custom-call(s32[2]{0:T(128)} %pad_add_fusion.me_ref, f32[256,768]{1,0:T(8,128)} %get-tuple-element.127.refs_0_, ...), custom_call_target="tpu_custom_call" | custom-call | flops 2415919104 | bytes 62914560 | tf_op jit(solution)/shard_map/columns_backward/pallas_call | solution.py:80
  220.1 8.2 %wide_weights.1 = (bf16[2,4,96,768]{3,2,1,0:T(8,128)(2,1)}, bf16[2,4,96,768]{3,2,1,0:T(8,128)(2,1)}, bf16[2,4,96,768]{3,2,1,0:T(8,128)(2,1)}, bf16[2,4,96,768]{3,2,1,0:T(8,128)(2,1)}) custom-call(s32[2]{0:T(128)} %pad_add_fusion.me_ref, bf16[2,256,768]{2,1,0:T(8,128)(2,1)} %get-tuple-element.135.left, ...), custom_call_target="tpu_custom_call" | custom-call | flops 2415919104 | bytes 62914560 | tf_op jit(solution)/shard_map/wide_weights/pallas_call | solution.py:80
  234.4 7.1 %column_weights.1 = (bf16[2,4,96,576]{3,2,1,0:T(8,128)(2,1)}, bf16[2,4,96,576]{3,2,1,0:T(8,128)(2,1)}, bf16[2,4,96,192]{3,2,1,0:T(8,128)(2,1)}, bf16[2,4,96,192]...) custom-call(s32[2]{0:T(128)} %pad_add_fusion.me_ref, ...), custom_call_target="tpu_custom_call" | custom-call | flops 1509949440 | bytes 25165824 | tf_op jit(solution)/shard_map/column_weights/pallas_call | solution.py:80
  241.5 7.6 %attend_back.1 = (bf16[8,64,512]{2,1,0:T(8,128)(2,1)}, f32[8,2,64,512]{3,2,1,0:T(8,128)}, bf16[8,2,64,512]{3,2,1,0:T(8,128)(2,1)}) custom-call(bf16[8,3,64,512]{3,2,1,0:T(8,128)(2,1)} %all-to-all-done.1.own, bf16[8,3,64,512]{3,2,1,0:T(8,128)(2,1)} %copy-done.44, f32[1,1024]{1,0:T(1,128)} %pad_maximum_fusion.11.key_ok, f32[512,1]{1,0:T(8,128)} %copy.40.weight, ...), custom_call_target="tpu_custom_call" | custom-call | flops 2684354560 | bytes 33554432 | tf_op jit(solution)/shard_map/attend_back/pallas_call | solution.py:80
  249.1 8.9 %collective-permute-done.30 = bf16[2,4,96,768]{3,2,1,0:T(8,128)(2,1)} collective-permute-done((bf16[2,4,96,768]{3,2,1,0:T(8,128)(2,1)}, bf16[2,4,96,768]{3,2,1,0:T(8,128)(2,1)}, u32[]{:S(2)}, u32[]{:S(2)}) %collective-permute-start.30) | collective-permute-done | bytes 1179680 | tf_op jit(solution)/shard_map/ppermute | solution.py:61
  265.4 10.3 %collective-permute-done.33 = bf16[1,4,96,768]{3,2,1,0:T(8,128)(2,1)S(1)} collective-permute-done((bf16[1,4,96,768]{3,2,1,0:T(8,128)(2,1)S(1)}, bf16[1,4,96,768]{3,2,1,0:T(8,128)(2,1)S(1)}, u32[]{:S(2)}, u32[]{:S(2)}) %collective-permute-start.33) | collective-permute-done | bytes 589856 | tf_op jit(solution)/shard_map/ppermute | solution.py:61
  289.9 9.5 %collective-permute-done.34 = bf16[96,1536]{1,0:T(8,128)(2,1)S(1)} collective-permute-done((bf16[96,1536]{1,0:T(8,128)(2,1)S(1)}, bf16[96,1536]{1,0:T(8,128)(2,1)S(1)}, u32[]{:S(2)}, u32[]{:S(2)}) %collective-permute-start.34) | collective-permute-done | bytes 294944 | tf_op jit(solution)/shard_map/ppermute | solution.py:61
  299.4 10.2 %collective-permute-done.35 = bf16[96,1536]{1,0:T(8,128)(2,1)S(1)} collective-permute-done((bf16[96,1536]{1,0:T(8,128)(2,1)S(1)}, bf16[96,1536]{1,0:T(8,128)(2,1)S(1)}, u32[]{:S(2)}, u32[]{:S(2)}) %collective-permute-start.35) | collective-permute-done | bytes 294944 | tf_op jit(solution)/shard_map/ppermute | solution.py:61
  316.1 7.3 %all-to-all-start.5 = ((bf16[4,576,256]{2,1,0:T(8,128)(2,1)}), bf16[4,576,256]{2,1,0:T(8,128)(2,1)S(1)}, u32[]{:S(2)}, u32[]{:S(2)}) async-start(bf16[4,576,256]{2,1,0:T(8,128)(2,1)} %get-tuple-element.162), calls=%async_computation.5 | async-start | bytes 2359296 | tf_op jit(solution)/shard_map/all_to_all | solution.py:69
  332.0 18.4 %collective-permute-done.40 = bf16[3,40,768]{2,1,0:T(8,128)(2,1)S(1)} collective-permute-done((bf16[3,40,768]{2,1,0:T(8,128)(2,1)S(1)}, bf16[3,40,768]{2,1,0:T(8,128)(2,1)S(1)}, u32[]{:S(2)}, u32[]{:S(2)}) %collective-permute-start.40) | collective-permute-done | bytes 184352 | tf_op jit(solution)/shard_map/ppermute | solution.py:61
  369.0 16.2 %collective-permute-done.43 = bf16[1,4,96,576]{3,2,1,0:T(8,128)(2,1)S(1)} collective-permute-done((bf16[1,4,96,576]{3,2,1,0:T(8,128)(2,1)S(1)}, bf16[1,4,96,576]{3,2,1,0:T(8,128)(2,1)S(1)}, u32[]{:S(2)}, u32[]{:S(2)}) %collective-permute-start.43) | collective-permute-done | bytes 442400 | tf_op jit(solution)/shard_map/ppermute | solution.py:61
  402.5 6.5 %finish.1 = bf16[256,768]{1,0:T(8,128)(2,1)} custom-call(s32[2]{0:T(128)} %pad_add_fusion.me_ref, bf16[4,576,256]{2,1,0:T(8,128)(2,1)} %copy-done.4, bf16[256,768]{1,0:T(8,128)(2,1)} %bitcast.91, f32[1,768]{1,0:T(1,128)} %broadcast_in_dim.29.refs_4_.gain.refs_2_, bf16[8,80,768]{2,1,0:T(8,128)(2,1)} %copy-done.2, bf16[8,80,768]{2,1,0:T(8,128)(2,1)} %bitcast.84, ...), custom_call_target="tpu_custom_call" | custom-call | flops 905969664 | bytes 16777216 | tf_op jit(solution)/shard_map/finish/pallas_call | solution.py:80
  409.0 6.2 %all-to-all-done.7 = bf16[4,112,960]{2,1,0:T(8,128)(2,1)S(1)} async-done(((bf16[4,112,960]{2,1,0:T(8,128)(2,1)}), bf16[4,112,960]{2,1,0:T(8,128)(2,1)S(1)}, u32[]{:S(2)}, u32[]{:S(2)}) %all-to-all-start.7) | async-done | bytes 860192 | tf_op jit(solution)/shard_map/all_to_all | solution.py:69
  (276 shorter events, 167.2 us)
Async XLA Ops:
  21.1 40.7 %all-to-all-start = ((bf16[8,2,32,768]{3,2,1,0:T(8,128)(2,1)}), bf16[8,2,32,768]{3,2,1,0:T(8,128)(2,1)S(1)}, u32[]{:S(2)}, u32[]{:S(2)}) async-start(bf16[8,2,32,768]{3,2,1,0:T(8,128)(2,1)} %pad_maximum_fusion.5), calls=%async_computation | async-start | bytes 1572864 | tf_op jit(solution)/shard_map/all_to_all | solution.py:69
  24.9 36.9 %collective-permute-start.6 = (bf16[3,128,768]{2,1,0:T(8,128)(2,1)S(1)}, bf16[3,128,768]{2,1,0:T(8,128)(2,1)S(1)}, u32[]{:S(2)}, u32[]{:S(2)}) collective-permute-start(bf16[3,128,768]{2,1,0:T(8,128)(2,1)S(1)} %pad_maximum_fusion.6), channel_id=1, source_target_pairs={{0,8},{8,0},{16,24},{24,16},{1,9},{9,1},{17,25},{25,17},{2,10},{10... | collective-permute-start | bytes 1769480 | tf_op jit(solution)/shard_map/ppermute | solution.py:61
  26.9 34.9 %collective-permute-start.7 = (bf16[3,128,768]{2,1,0:T(8,128)(2,1)S(1)}, bf16[3,128,768]{2,1,0:T(8,128)(2,1)S(1)}, u32[]{:S(2)}, u32[]{:S(2)}) collective-permute-start(bf16[3,128,768]{2,1,0:T(8,128)(2,1)S(1)} %pad_maximum_fusion.6), channel_id=1, source_target_pairs={{0,16},{8,24},{16,0},{24,8},{1,17},{9,25},{17,1},{25,9},{2,18},{10... | collective-permute-start | bytes 1769480 | tf_op jit(solution)/shard_map/ppermute | solution.py:61
  32.0 29.8 %collective-permute-start.4 = (bf16[256,768]{1,0:T(8,128)(2,1)S(1)}, bf16[256,768]{1,0:T(8,128)(2,1)}, u32[]{:S(2)}, u32[]{:S(2)}) collective-permute-start(bf16[256,768]{1,0:T(8,128)(2,1)S(1)} %bitcast.94), channel_id=1, source_target_pairs={{0,2},{1,3},{2,0},{3,1},{4,6},{5,7},{6,4},{7,5},{8,10},{9,11},{10,... | collective-permute-start | bytes 1179656 | tf_op jit(solution)/shard_map/ppermute | solution.py:61
  33.9 27.9 %collective-permute-start.5 = (bf16[256,768]{1,0:T(8,128)(2,1)S(1)}, bf16[256,768]{1,0:T(8,128)(2,1)}, u32[]{:S(2)}, u32[]{:S(2)}) collective-permute-start(bf16[256,768]{1,0:T(8,128)(2,1)S(1)} %bitcast.95), channel_id=1, source_target_pairs={{0,3},{1,2},{2,1},{3,0},{4,7},{5,6},{6,5},{7,4},{8,11},{9,10},{10,... | collective-permute-start | bytes 1179656 | tf_op jit(solution)/shard_map/ppermute | solution.py:61
  67.1 35.7 %all-to-all-start.1 = ((bf16[8,3,64,512]{3,2,1,0:T(8,128)(2,1)}), bf16[8,3,64,512]{3,2,1,0:T(8,128)(2,1)}, u32[]{:S(2)}, u32[]{:S(2)}) async-start(bf16[8,3,64,512]{3,2,1,0:T(8,128)(2,1)} %get-tuple-element.107), calls=%async_computation.1 | async-start | bytes 3145728 | tf_op jit(solution)/shard_map/all_to_all | solution.py:69
  79.2 23.5 %collective-permute-start.9 = (bf16[192,768]{1,0:T(8,128)(2,1)S(1)}, bf16[192,768]{1,0:T(8,128)(2,1)S(1)}, u32[]{:S(2)}, u32[]{:S(2)}) collective-permute-start(bf16[192,768]{1,0:T(8,128)(2,1)S(1)} %dynamic-slice_bitcast_fusion), channel_id=1, source_target_pairs={{0,2},{1,3},{2,0},{3,1},{4,6},{5,7},{6,4},{7,5},{8,10},{9,11},{10,... | collective-permute-start | bytes 884744 | tf_op jit(solution)/shard_map/ppermute | solution.py:61
  131.1 28.3 %all-to-all-start.2 = ((bf16[16,32,512]{2,1,0:T(8,128)(2,1)}), bf16[16,32,512]{2,1,0:T(8,128)(2,1)S(1)}, u32[]{:S(2)}, u32[]{:S(2)}) async-start(bf16[16,32,512]{2,1,0:T(8,128)(2,1)} %attend.1), calls=%async_computation.2 | async-start | bytes 1048576 | tf_op jit(solution)/shard_map/all_to_all | solution.py:69
  190.6 29.5 %collective-permute-start.24 = (bf16[2,4,256,768]{3,2,1,0:T(8,128)(2,1)}, bf16[2,4,256,768]{3,2,1,0:T(8,128)(2,1)}, u32[]{:S(2)}, u32[]{:S(2)}) collective-permute-start(bf16[2,4,256,768]{3,2,1,0:T(8,128)(2,1)} %get-tuple-element.136.right), channel_id=1, source_target_pairs={{0,4},{4,0},{1,5},{5,1},{2,6},{6,2},{3,7},{7,3},{8,12},{12,8},{9,1... | collective-permute-start | bytes 9437192 | tf_op jit(solution)/shard_map/ppermute | solution.py:61
  207.8 25.3 %collective-permute-start.26 = (bf16[4,256,1024]{2,1,0:T(8,128)(2,1)}, bf16[4,256,1024]{2,1,0:T(8,128)(2,1)S(1)}, u32[]{:S(2)}, u32[]{:S(2)}) collective-permute-start(bf16[4,256,1024]{2,1,0:T(8,128)(2,1)} %get-tuple-element.139.right), channel_id=1, source_target_pairs={{0,4},{4,0},{1,5},{5,1},{2,6},{6,2},{3,7},{7,3},{8,12},{12,8},{9,1... | collective-permute-start | bytes 6291464 | tf_op jit(solution)/shard_map/ppermute | solution.py:61
  208.4 24.7 %collective-permute-start.25 = (bf16[3,256,768]{2,1,0:T(8,128)(2,1)}, bf16[3,256,768]{2,1,0:T(8,128)(2,1)}, u32[]{:S(2)}, u32[]{:S(2)}) collective-permute-start(bf16[3,256,768]{2,1,0:T(8,128)(2,1)} %get-tuple-element.138.left), channel_id=1, source_target_pairs={{0,4},{4,0},{1,5},{5,1},{2,6},{6,2},{3,7},{7,3},{8,12},{12,8},{9,1... | collective-permute-start | bytes 3538952 | tf_op jit(solution)/shard_map/ppermute | solution.py:61
  214.6 27.0 %all-to-all-start.3 = ((bf16[16,32,512]{2,1,0:T(8,128)(2,1)}), bf16[16,32,512]{2,1,0:T(8,128)(2,1)}, u32[]{:S(2)}, u32[]{:S(2)}) async-start(bf16[16,32,512]{2,1,0:T(8,128)(2,1)} %bitcast.102), calls=%async_computation.3 | async-start | bytes 1048576 | tf_op jit(solution)/shard_map/all_to_all | solution.py:69
  228.3 29.7 %collective-permute-start.30 = (bf16[2,4,96,768]{3,2,1,0:T(8,128)(2,1)}, bf16[2,4,96,768]{3,2,1,0:T(8,128)(2,1)}, u32[]{:S(2)}, u32[]{:S(2)}) collective-permute-start(bf16[2,4,96,768]{3,2,1,0:T(8,128)(2,1)} %get-tuple-element.151), channel_id=1, source_target_pairs={{0,8},{8,0},{16,24},{24,16},{1,9},{9,1},{17,25},{25,17},{2,10},{10... | collective-permute-start | bytes 3538952 | tf_op jit(solution)/shard_map/ppermute | solution.py:61
  230.4 28.2 %collective-permute-start.29 = (bf16[2,4,96,768]{3,2,1,0:T(8,128)(2,1)}, bf16[2,4,96,768]{3,2,1,0:T(8,128)(2,1)}, u32[]{:S(2)}, u32[]{:S(2)}) collective-permute-start(bf16[2,4,96,768]{3,2,1,0:T(8,128)(2,1)} %get-tuple-element.150), channel_id=1, source_target_pairs={{0,16},{8,24},{16,0},{24,8},{1,17},{9,25},{17,1},{25,9},{2,18},{10... | collective-permute-start | bytes 3538952 | tf_op jit(solution)/shard_map/ppermute | solution.py:61
  278.1 32.3 %all-to-all-start.4 = ((bf16[8,3,64,512]{3,2,1,0:T(8,128)(2,1)}), bf16[8,3,64,512]{3,2,1,0:T(8,128)(2,1)S(1)}, u32[]{:S(2)}, u32[]{:S(2)}) async-start(bf16[8,3,64,512]{3,2,1,0:T(8,128)(2,1)} %pad_maximum_fusion.1), calls=%async_computation.4 | async-start | bytes 3145728 | tf_op jit(solution)/shard_map/all_to_all | solution.py:69
  286.1 23.5 %collective-permute-start.35 = (bf16[96,1536]{1,0:T(8,128)(2,1)S(1)}, bf16[96,1536]{1,0:T(8,128)(2,1)S(1)}, u32[]{:S(2)}, u32[]{:S(2)}) collective-permute-start(bf16[96,1536]{1,0:T(8,128)(2,1)S(1)} %get-tuple-element.221), channel_id=1, source_target_pairs={{0,2},{1,3},{2,0},{3,1},{4,6},{5,7},{6,4},{7,5},{8,10},{9,11},{10,... | collective-permute-start | bytes 884744 | tf_op jit(solution)/shard_map/ppermute | solution.py:61
  316.1 37.3 %all-to-all-start.5 = ((bf16[4,576,256]{2,1,0:T(8,128)(2,1)}), bf16[4,576,256]{2,1,0:T(8,128)(2,1)S(1)}, u32[]{:S(2)}, u32[]{:S(2)}) async-start(bf16[4,576,256]{2,1,0:T(8,128)(2,1)} %get-tuple-element.162), calls=%async_computation.5 | async-start | bytes 2359296 | tf_op jit(solution)/shard_map/all_to_all | solution.py:69
  323.4 30.0 %collective-permute-start.37 = (bf16[2,4,96,576]{3,2,1,0:T(8,128)(2,1)}, bf16[2,4,96,576]{3,2,1,0:T(8,128)(2,1)}, u32[]{:S(2)}, u32[]{:S(2)}) collective-permute-start(bf16[2,4,96,576]{3,2,1,0:T(8,128)(2,1)} %get-tuple-element.163), channel_id=1, source_target_pairs={{0,16},{8,24},{16,0},{24,8},{1,17},{9,25},{17,1},{25,9},{2,18},{10... | collective-permute-start | bytes 2654216 | tf_op jit(solution)/shard_map/ppermute | solution.py:61
  325.9 25.8 %collective-permute-start.39 = (bf16[4,96,576]{2,1,0:T(8,128)(2,1)}, bf16[4,96,576]{2,1,0:T(8,128)(2,1)S(1)}, u32[]{:S(2)}, u32[]{:S(2)}) collective-permute-start(bf16[4,96,576]{2,1,0:T(8,128)(2,1)} %get-tuple-element.165), channel_id=1, source_target_pairs={{0,4},{4,0},{1,5},{5,1},{2,6},{6,2},{3,7},{7,3},{8,12},{12,8},{9,1... | collective-permute-start | bytes 1327112 | tf_op jit(solution)/shard_map/ppermute | solution.py:61
  325.9 25.8 %collective-permute-start.38 = (bf16[2,4,96,384]{3,2,1,0:T(8,128)(2,1)}, bf16[2,4,96,384]{3,2,1,0:T(8,128)(2,1)S(1)}, u32[]{:S(2)}, u32[]{:S(2)}) collective-permute-start(bf16[2,4,96,384]{3,2,1,0:T(8,128)(2,1)} %pad_maximum_fusion.7), channel_id=1, source_target_pairs={{0,8},{8,0},{16,24},{24,16},{1,9},{9,1},{17,25},{25,17},{2,10},{10... | collective-permute-start | bytes 1769480 | tf_op jit(solution)/shard_map/ppermute | solution.py:61
  351.8 50.8 %collective-permute-start.42 = (bf16[3,320,768]{2,1,0:T(8,128)(2,1)}, bf16[3,320,768]{2,1,0:T(8,128)(2,1)}, u32[]{:S(2)}, u32[]{:S(2)}) collective-permute-start(bf16[3,320,768]{2,1,0:T(8,128)(2,1)} %constant_dynamic-update-slice_fusion.10.refs_5_), channel_id=1, source_target_pairs={{0,4},{4,0},{1,5},{5,1},{2,6},{6,2},{3,7},{7,3},{8,12},{12,8},{9,1... | collective-permute-start | bytes 4423688 | tf_op jit(solution)/shard_map/ppermute | solution.py:61
  357.4 29.0 %all-to-all-start.6 = ((bf16[8,80,768]{2,1,0:T(8,128)(2,1)}), bf16[8,80,768]{2,1,0:T(8,128)(2,1)S(1)}, u32[]{:S(2)}, u32[]{:S(2)}) async-start(bf16[8,80,768]{2,1,0:T(8,128)(2,1)} %pad_maximum_fusion.2), calls=%async_computation.6 | async-start | bytes 1966080 | tf_op jit(solution)/shard_map/all_to_all | solution.py:69
  366.4 27.5 %collective-permute-start.45 = (bf16[2,96,576]{2,1,0:T(8,128)(2,1)}, bf16[2,96,576]{2,1,0:T(8,128)(2,1)}, u32[]{:S(2)}, u32[]{:S(2)}) collective-permute-start(bf16[2,96,576]{2,1,0:T(8,128)(2,1)} %get-tuple-element.223), channel_id=1, source_target_pairs={{0,16},{8,24},{16,0},{24,8},{1,17},{9,25},{17,1},{25,9},{2,18},{10... | collective-permute-start | bytes 663560 | tf_op jit(solution)/shard_map/ppermute | solution.py:61
  387.7 27.5 %all-to-all-start.7 = ((bf16[4,112,960]{2,1,0:T(8,128)(2,1)}), bf16[4,112,960]{2,1,0:T(8,128)(2,1)S(1)}, u32[]{:S(2)}, u32[]{:S(2)}) async-start(bf16[4,112,960]{2,1,0:T(8,128)(2,1)} %pad_maximum_fusion.3), calls=%async_computation.7 | async-start | bytes 1835008 | tf_op jit(solution)/shard_map/all_to_all | solution.py:69
  (77 other events, 887.6 us)

commit v2 on v1

--- a/solution.py
+++ b/solution.py
@@ -846,11 +846,12 @@
     gains = jnp.concatenate([row_gain_grad, col_gain_grad, ffn_gain_grad], axis=0)
     home = home.reshape(seqs, 2 * few, width)
     if fast:
+        traded, qkv_came, outs_came = together(traded, qkv_came, outs_came)
         traded = exchange(traded, "tp")
+        (qkv_kept, qkv_sent), (outs_kept, outs_sent) = halve(qkv_kept, qkv_came), halve(outs_kept, outs_came)
+        qkv_came, outs_came = give(qkv_sent, 1), give(outs_sent, 2)
         came = swap(sent, "r", ranks, 1)
         home, traded, qkv_came, outs_came, came = together(home, traded, qkv_came, outs_came, came)
-        (qkv_kept, qkv_sent), (outs_kept, outs_sent) = halve(qkv_kept, qkv_came), halve(outs_kept, outs_came)
-        qkv_came, outs_came = give(qkv_sent, 1), give(outs_sent, 2)
         ends = jnp.broadcast_to(two_terms(gains), (seqs, 16, width))
         home = exchange(jnp.concatenate([home, ends], axis=1), SEQ)
         gains = one_term(jnp.sum(home[:, 2 * few :].astype(F32), axis=0))

time: 425 us -> 425 us (level)
    ppermute x47, waiting for transfers between devices: 162 us -> 151 us  [swap(): return lax.ppermute(value, axis, [(i, i ^ mask) for i in range(size)])]
    all_to_all x8, waiting for transfers between devices: 6.25 us -> 16.4 us  [exchange(): return lax.all_to_all(value, axis, split_axis=0, concat_axis=0, tiled=True)]
    unnamed x108, local copies, waits for them, and re-layouts: 18.6 us -> 13.6 us
  transfers between devices with their start and end apart: 55 -> 55, of which waited for: 22 -> 26; matrix products, arithmetic and copies ran while one was open for 10% -> 10% of each run, Pallas kernels for 15% -> 16%
where the time goes in v2:
time: 425 us; the launch traced here: 418 us
  waiting for transfers between devices  168 us (40%)
  starting transfers between devices  110 us (26%)
  Pallas kernels  84.5 us (20%)
  local copies, waits for them, and re-layouts  26.9 us (6%)
  other arithmetic  26 us (6%)
    ppermute x47, waiting for transfers between devices, swap(): return lax.ppermute(value, axis, [(i, i ^ mask) for i in range(size)])  151 us
    pallas_call x10, Pallas kernels, call(): pl.pallas_call(body, out_shape=[jax.ShapeDtypeStruct(shape, kind) for sha...  84.5 us
    ppermute x47, starting transfers between devices, swap(): return lax.ppermute(value, axis, [(i, i ^ mask) for i in range(size)])  66.1 us
    all_to_all x8, starting transfers between devices, exchange(): return lax.all_to_all(value, axis, split_axis=0, concat_axis=0, tiled=True)  44.3 us
    all_to_all x8, waiting for transfers between devices, exchange(): return lax.all_to_all(value, axis, split_axis=0, concat_axis=0, tiled=True)  16.4 us
    unnamed x108, local copies, waits for them, and re-layouts  13.6 us
  transfers between devices with their start and end apart: 55, of which 26 were waited for; matrix products, arithmetic and copies ran while one was open for 10% of the time, Pallas kernels for 16%

profile of v2, /device:TPU:0, one launch (start us, length us, event | category | flops | bytes accessed | tf_op | source)
XLA Modules:
  0.0 418.0 jit_solution(6369317118043657947)
XLA Ops:
  8.9 11.7 %collective-permute-done.1 = bf16[128,768]{1,0:T(8,128)(2,1)S(1)} collective-permute-done((bf16[128,768]{1,0:T(8,128)(2,1)S(1)}, bf16[128,768]{1,0:T(8,128)(2,1)S(1)}, u32[]{:S(2)}, u32[]{:S(2)}) %collective-permute-start.1) | collective-permute-done | bytes 196640 | tf_op jit(solution)/shard_map/ppermute | solution.py:61
  36.6 12.2 %collective-permute-done.3.refs_1_ = bf16[256,768]{1,0:T(8,128)(2,1)S(1)} collective-permute-done((bf16[256,768]{1,0:T(8,128)(2,1)S(1)}, bf16[256,768]{1,0:T(8,128)(2,1)S(1)}, u32[]{:S(2)}, u32[]{:S(2)}) %collective-permute-start.3) | collective-permute-done | bytes 393248 | tf_op jit(solution)/shard_map/ppermute | solution.py:61
  48.8 13.0 %collective-permute-done.4.refs_2_ = bf16[256,768]{1,0:T(8,128)(2,1)} collective-permute-done((bf16[256,768]{1,0:T(8,128)(2,1)S(1)}, bf16[256,768]{1,0:T(8,128)(2,1)}, u32[]{:S(2)}, u32[]{:S(2)}) %collective-permute-start.4) | collective-permute-done | bytes 393248 | tf_op jit(solution)/shard_map/ppermute | solution.py:61
  71.8 7.4 %collective-permute-start.8 = (bf16[192,768]{1,0:T(8,128)(2,1)S(1)}, bf16[192,768]{1,0:T(8,128)(2,1)S(1)}, u32[]{:S(2)}, u32[]{:S(2)}) collective-permute-start(bf16[192,768]{1,0:T(8,128)(2,1)S(1)} %dynamic-slice_bitcast_fusion), channel_id=1, source_target_pairs={{0,1},{1,0},{2,3},{3,2},{4,5},{5,4},{6,7},{7,6},{8,9},{9,8},{10,11... | collective-permute-start | bytes 884744 | tf_op jit(solution)/shard_map/ppermute | solution.py:61
  86.3 6.7 %collective-permute-done.8 = bf16[192,768]{1,0:T(8,128)(2,1)S(1)} collective-permute-done((bf16[192,768]{1,0:T(8,128)(2,1)S(1)}, bf16[192,768]{1,0:T(8,128)(2,1)S(1)}, u32[]{:S(2)}, u32[]{:S(2)}) %collective-permute-start.8) | collective-permute-done | bytes 294944 | tf_op jit(solution)/shard_map/ppermute | solution.py:61
  93.0 9.7 %collective-permute-done.9 = bf16[192,768]{1,0:T(8,128)(2,1)S(1)} collective-permute-done((bf16[192,768]{1,0:T(8,128)(2,1)S(1)}, bf16[192,768]{1,0:T(8,128)(2,1)S(1)}, u32[]{:S(2)}, u32[]{:S(2)}) %collective-permute-start.9) | collective-permute-done | bytes 294944 | tf_op jit(solution)/shard_map/ppermute | solution.py:61
  117.1 12.5 %collective-permute-done.15 = bf16[3,192,768]{2,1,0:T(8,128)(2,1)} collective-permute-done((bf16[3,192,768]{2,1,0:T(8,128)(2,1)S(1)}, bf16[3,192,768]{2,1,0:T(8,128)(2,1)}, u32[]{:S(2)}, u32[]{:S(2)}) %collective-permute-start.15) | collective-permute-done | bytes 884768 | tf_op jit(solution)/shard_map/ppermute | solution.py:61
  131.1 10.3 %all-to-all-start.2 = ((bf16[16,32,512]{2,1,0:T(8,128)(2,1)}), bf16[16,32,512]{2,1,0:T(8,128)(2,1)S(1)}, u32[]{:S(2)}, u32[]{:S(2)}) async-start(bf16[16,32,512]{2,1,0:T(8,128)(2,1)} %attend.1), calls=%async_computation.2 | async-start | bytes 1048576 | tf_op jit(solution)/shard_map/all_to_all | solution.py:69
  149.6 8.6 %collective-permute-done.17 = bf16[3,96,768]{2,1,0:T(8,128)(2,1)S(1)} collective-permute-done((bf16[3,96,768]{2,1,0:T(8,128)(2,1)S(1)}, bf16[3,96,768]{2,1,0:T(8,128)(2,1)S(1)}, u32[]{:S(2)}, u32[]{:S(2)}) %collective-permute-start.17) | collective-permute-done | bytes 442400 | tf_op jit(solution)/shard_map/ppermute | solution.py:61
  166.8 12.6 %columns_forward.1 = (f32[256,768]{1,0:T(8,128)}, bf16[256,768]{1,0:T(8,128)(2,1)}, bf16[3,4,256,192]{3,2,1,0:T(8,128)(2,1)}, bf16[4,256,1024]{2,1,0:T(8,128)(2,1)}, f32[256,768]{1,0:T(8,128)}) custom-call(s32[2]{0:T(128)} %pad_add_fusion.me_ref, bf16[8,2,32,768]{3,2,1,0:T(8,128)(2,1)} %copy-done.7, bf16[4,4,32,512]{3,2,1,0:T(8,128)(2,1)} %bitcast.89, ...), custom_call_target="tpu_custom_call" | custom-call | flops 1509949440 | bytes 41943040 | tf_op jit(solution)/shard_map/columns_forward/pallas_call | solution.py:80
  179.5 11.1 %feed_forward.1 = (bf16[256,768]{1,0:T(8,128)(2,1)}, f32[256,768]{1,0:T(8,128)}, f32[1,768]{1,0:T(1,128)}, bf16[2,256,768]{2,1,0:T(8,128)(2,1)}, bf16[2,4,256,768]{3,2,1,0:T(8,128)(2,1)}) custom-call(s32[2]{0:T(128)} %pad_add_fusion.me_ref, f32[256,768]{1,0:T(8,128)} %get-tuple-element.127.after_col, bf16[8,2,32,768]{3,2,1,0:T(8,128)(2,1)} %copy-done.7, ...), custom_call_target="tpu_custom_call" | custom-call | flops 4831838208 | bytes 62914560 | tf_op jit(solution)/shard_map/feed_forward/pallas_call | solution.py:80
  190.7 17.1 %columns_backward.1 = (bf16[8,2,32,768]{3,2,1,0:T(8,128)(2,1)}, bf16[3,256,768]{2,1,0:T(8,128)(2,1)}, bf16[4,256,1024]{2,1,0:T(8,128)(2,1)}, bf16[4,4,32,512]{3,2,1,0:T(8,128)(2,1)}, f32[1,768]{1,0:T(1,128)}) custom-call(s32[2]{0:T(128)} %pad_add_fusion.me_ref, f32[256,768]{1,0:T(8,128)} %get-tuple-element.130.refs_0_, ...), custom_call_target="tpu_custom_call" | custom-call | flops 2415919104 | bytes 62914560 | tf_op jit(solution)/shard_map/columns_backward/pallas_call | solution.py:80
  220.1 8.2 %wide_weights.1 = (bf16[2,4,96,768]{3,2,1,0:T(8,128)(2,1)}, bf16[2,4,96,768]{3,2,1,0:T(8,128)(2,1)}, bf16[2,4,96,768]{3,2,1,0:T(8,128)(2,1)}, bf16[2,4,96,768]{3,2,1,0:T(8,128)(2,1)}) custom-call(s32[2]{0:T(128)} %pad_add_fusion.me_ref, bf16[2,256,768]{2,1,0:T(8,128)(2,1)} %get-tuple-element.138.left, ...), custom_call_target="tpu_custom_call" | custom-call | flops 2415919104 | bytes 62914560 | tf_op jit(solution)/shard_map/wide_weights/pallas_call | solution.py:80
  234.4 7.1 %column_weights.1 = (bf16[2,4,96,576]{3,2,1,0:T(8,128)(2,1)}, bf16[2,4,96,576]{3,2,1,0:T(8,128)(2,1)}, bf16[2,4,96,192]{3,2,1,0:T(8,128)(2,1)}, bf16[2,4,96,192]...) custom-call(s32[2]{0:T(128)} %pad_add_fusion.me_ref, ...), custom_call_target="tpu_custom_call" | custom-call | flops 1509949440 | bytes 25165824 | tf_op jit(solution)/shard_map/column_weights/pallas_call | solution.py:80
  241.5 7.6 %attend_back.1 = (bf16[8,64,512]{2,1,0:T(8,128)(2,1)}, f32[8,2,64,512]{3,2,1,0:T(8,128)}, bf16[8,2,64,512]{3,2,1,0:T(8,128)(2,1)}) custom-call(bf16[8,3,64,512]{3,2,1,0:T(8,128)(2,1)} %all-to-all-done.1.own, bf16[8,3,64,512]{3,2,1,0:T(8,128)(2,1)} %copy-done.44, f32[1,1024]{1,0:T(1,128)} %pad_maximum_fusion.11.key_ok, f32[512,1]{1,0:T(8,128)} %copy.40.weight, ...), custom_call_target="tpu_custom_call" | custom-call | flops 2684354560 | bytes 33554432 | tf_op jit(solution)/shard_map/attend_back/pallas_call | solution.py:80
  249.1 8.9 %collective-permute-done.30 = bf16[2,4,96,768]{3,2,1,0:T(8,128)(2,1)} collective-permute-done((bf16[2,4,96,768]{3,2,1,0:T(8,128)(2,1)}, bf16[2,4,96,768]{3,2,1,0:T(8,128)(2,1)}, u32[]{:S(2)}, u32[]{:S(2)}) %collective-permute-start.30) | collective-permute-done | bytes 1179680 | tf_op jit(solution)/shard_map/ppermute | solution.py:61
  265.4 10.3 %collective-permute-done.33 = bf16[1,4,96,768]{3,2,1,0:T(8,128)(2,1)S(1)} collective-permute-done((bf16[1,4,96,768]{3,2,1,0:T(8,128)(2,1)S(1)}, bf16[1,4,96,768]{3,2,1,0:T(8,128)(2,1)S(1)}, u32[]{:S(2)}, u32[]{:S(2)}) %collective-permute-start.33) | collective-permute-done | bytes 589856 | tf_op jit(solution)/shard_map/ppermute | solution.py:61
  289.9 9.5 %collective-permute-done.34 = bf16[96,1536]{1,0:T(8,128)(2,1)S(1)} collective-permute-done((bf16[96,1536]{1,0:T(8,128)(2,1)S(1)}, bf16[96,1536]{1,0:T(8,128)(2,1)S(1)}, u32[]{:S(2)}, u32[]{:S(2)}) %collective-permute-start.34) | collective-permute-done | bytes 294944 | tf_op jit(solution)/shard_map/ppermute | solution.py:61
  299.4 10.2 %collective-permute-done.35 = bf16[96,1536]{1,0:T(8,128)(2,1)S(1)} collective-permute-done((bf16[96,1536]{1,0:T(8,128)(2,1)S(1)}, bf16[96,1536]{1,0:T(8,128)(2,1)S(1)}, u32[]{:S(2)}, u32[]{:S(2)}) %collective-permute-start.35) | collective-permute-done | bytes 294944 | tf_op jit(solution)/shard_map/ppermute | solution.py:61
  324.5 7.4 %collective-permute-done.37 = bf16[2,4,96,576]{3,2,1,0:T(8,128)(2,1)} collective-permute-done((bf16[2,4,96,576]{3,2,1,0:T(8,128)(2,1)}, bf16[2,4,96,576]{3,2,1,0:T(8,128)(2,1)}, u32[]{:S(2)}, u32[]{:S(2)}) %collective-permute-start.37) | collective-permute-done | bytes 884768 | tf_op jit(solution)/shard_map/ppermute | solution.py:61
  331.9 9.2 %all-to-all-start.5 = ((bf16[4,576,256]{2,1,0:T(8,128)(2,1)}), bf16[4,576,256]{2,1,0:T(8,128)(2,1)S(1)}, u32[]{:S(2)}, u32[]{:S(2)}) async-start(bf16[4,576,256]{2,1,0:T(8,128)(2,1)} %get-tuple-element.168), calls=%async_computation.5 | async-start | bytes 2359296 | tf_op jit(solution)/shard_map/all_to_all | solution.py:69
  350.6 7.7 %collective-permute-done.40 = bf16[1,4,96,384]{3,2,1,0:T(8,128)(2,1)S(1)} collective-permute-done((bf16[1,4,96,384]{3,2,1,0:T(8,128)(2,1)S(1)}, bf16[1,4,96,384]{3,2,1,0:T(8,128)(2,1)S(1)}, u32[]{:S(2)}, u32[]{:S(2)}) %collective-permute-start.40) | collective-permute-done | bytes 294944 | tf_op jit(solution)/shard_map/ppermute | solution.py:61
  361.9 6.4 %all-to-all-done.5.refs_0_ = bf16[4,576,256]{2,1,0:T(8,128)(2,1)S(1)} async-done(((bf16[4,576,256]{2,1,0:T(8,128)(2,1)}), bf16[4,576,256]{2,1,0:T(8,128)(2,1)S(1)}, u32[]{:S(2)}, u32[]{:S(2)}) %all-to-all-start.5) | async-done | bytes 1179680 | tf_op jit(solution)/shard_map/all_to_all | solution.py:69
  404.0 6.5 %finish.1 = bf16[256,768]{1,0:T(8,128)(2,1)} custom-call(s32[2]{0:T(128)} %pad_add_fusion.me_ref, bf16[4,576,256]{2,1,0:T(8,128)(2,1)} %copy-done.4, bf16[256,768]{1,0:T(8,128)(2,1)} %bitcast.91, f32[1,768]{1,0:T(1,128)} %broadcast_in_dim.29.refs_4_.gain.refs_2_, bf16[8,80,768]{2,1,0:T(8,128)(2,1)} %copy-done.2, bf16[8,80,768]{2,1,0:T(8,128)(2,1)} %bitcast.84, ...), custom_call_target="tpu_custom_call" | custom-call | flops 905969664 | bytes 16777216 | tf_op jit(solution)/shard_map/finish/pallas_call | solution.py:80
  (276 shorter events, 183.6 us)
Async XLA Ops:
  21.1 40.7 %all-to-all-start = ((bf16[8,2,32,768]{3,2,1,0:T(8,128)(2,1)}), bf16[8,2,32,768]{3,2,1,0:T(8,128)(2,1)S(1)}, u32[]{:S(2)}, u32[]{:S(2)}) async-start(bf16[8,2,32,768]{3,2,1,0:T(8,128)(2,1)} %pad_maximum_fusion.5), calls=%async_computation | async-start | bytes 1572864 | tf_op jit(solution)/shard_map/all_to_all | solution.py:69
  24.9 36.9 %collective-permute-start.6 = (bf16[3,128,768]{2,1,0:T(8,128)(2,1)S(1)}, bf16[3,128,768]{2,1,0:T(8,128)(2,1)S(1)}, u32[]{:S(2)}, u32[]{:S(2)}) collective-permute-start(bf16[3,128,768]{2,1,0:T(8,128)(2,1)S(1)} %pad_maximum_fusion.6), channel_id=1, source_target_pairs={{0,8},{8,0},{16,24},{24,16},{1,9},{9,1},{17,25},{25,17},{2,10},{10... | collective-permute-start | bytes 1769480 | tf_op jit(solution)/shard_map/ppermute | solution.py:61
  26.9 34.9 %collective-permute-start.7 = (bf16[3,128,768]{2,1,0:T(8,128)(2,1)S(1)}, bf16[3,128,768]{2,1,0:T(8,128)(2,1)S(1)}, u32[]{:S(2)}, u32[]{:S(2)}) collective-permute-start(bf16[3,128,768]{2,1,0:T(8,128)(2,1)S(1)} %pad_maximum_fusion.6), channel_id=1, source_target_pairs={{0,16},{8,24},{16,0},{24,8},{1,17},{9,25},{17,1},{25,9},{2,18},{10... | collective-permute-start | bytes 1769480 | tf_op jit(solution)/shard_map/ppermute | solution.py:61
  32.0 29.8 %collective-permute-start.4 = (bf16[256,768]{1,0:T(8,128)(2,1)S(1)}, bf16[256,768]{1,0:T(8,128)(2,1)}, u32[]{:S(2)}, u32[]{:S(2)}) collective-permute-start(bf16[256,768]{1,0:T(8,128)(2,1)S(1)} %bitcast.94), channel_id=1, source_target_pairs={{0,2},{1,3},{2,0},{3,1},{4,6},{5,7},{6,4},{7,5},{8,10},{9,11},{10,... | collective-permute-start | bytes 1179656 | tf_op jit(solution)/shard_map/ppermute | solution.py:61
  33.9 27.9 %collective-permute-start.5 = (bf16[256,768]{1,0:T(8,128)(2,1)S(1)}, bf16[256,768]{1,0:T(8,128)(2,1)}, u32[]{:S(2)}, u32[]{:S(2)}) collective-permute-start(bf16[256,768]{1,0:T(8,128)(2,1)S(1)} %bitcast.95), channel_id=1, source_target_pairs={{0,3},{1,2},{2,1},{3,0},{4,7},{5,6},{6,5},{7,4},{8,11},{9,10},{10,... | collective-permute-start | bytes 1179656 | tf_op jit(solution)/shard_map/ppermute | solution.py:61
  67.1 35.7 %all-to-all-start.1 = ((bf16[8,3,64,512]{3,2,1,0:T(8,128)(2,1)}), bf16[8,3,64,512]{3,2,1,0:T(8,128)(2,1)}, u32[]{:S(2)}, u32[]{:S(2)}) async-start(bf16[8,3,64,512]{3,2,1,0:T(8,128)(2,1)} %get-tuple-element.110), calls=%async_computation.1 | async-start | bytes 3145728 | tf_op jit(solution)/shard_map/all_to_all | solution.py:69
  79.2 23.5 %collective-permute-start.9 = (bf16[192,768]{1,0:T(8,128)(2,1)S(1)}, bf16[192,768]{1,0:T(8,128)(2,1)S(1)}, u32[]{:S(2)}, u32[]{:S(2)}) collective-permute-start(bf16[192,768]{1,0:T(8,128)(2,1)S(1)} %dynamic-slice_bitcast_fusion), channel_id=1, source_target_pairs={{0,2},{1,3},{2,0},{3,1},{4,6},{5,7},{6,4},{7,5},{8,10},{9,11},{10,... | collective-permute-start | bytes 884744 | tf_op jit(solution)/shard_map/ppermute | solution.py:61
  107.7 21.9 %collective-permute-start.15 = (bf16[3,192,768]{2,1,0:T(8,128)(2,1)S(1)}, bf16[3,192,768]{2,1,0:T(8,128)(2,1)}, u32[]{:S(2)}, u32[]{:S(2)}) collective-permute-start(bf16[3,192,768]{2,1,0:T(8,128)(2,1)S(1)} %pad_maximum_fusion.4), channel_id=1, source_target_pairs={{0,8},{8,0},{16,24},{24,16},{1,9},{9,1},{17,25},{25,17},{2,10},{10... | collective-permute-start | bytes 2654216 | tf_op jit(solution)/shard_map/ppermute | solution.py:61
  109.6 21.5 %collective-permute-start.16 = (bf16[3,192,768]{2,1,0:T(8,128)(2,1)S(1)}, bf16[3,192,768]{2,1,0:T(8,128)(2,1)}, u32[]{:S(2)}, u32[]{:S(2)}) collective-permute-start(bf16[3,192,768]{2,1,0:T(8,128)(2,1)S(1)} %pad_maximum_fusion.4), channel_id=1, source_target_pairs={{0,16},{8,24},{16,0},{24,8},{1,17},{9,25},{17,1},{25,9},{2,18},{10... | collective-permute-start | bytes 2654216 | tf_op jit(solution)/shard_map/ppermute | solution.py:61
  131.1 28.3 %all-to-all-start.2 = ((bf16[16,32,512]{2,1,0:T(8,128)(2,1)}), bf16[16,32,512]{2,1,0:T(8,128)(2,1)S(1)}, u32[]{:S(2)}, u32[]{:S(2)}) async-start(bf16[16,32,512]{2,1,0:T(8,128)(2,1)} %attend.1), calls=%async_computation.2 | async-start | bytes 1048576 | tf_op jit(solution)/shard_map/all_to_all | solution.py:69
  190.6 29.5 %collective-permute-start.24 = (bf16[2,4,256,768]{3,2,1,0:T(8,128)(2,1)}, bf16[2,4,256,768]{3,2,1,0:T(8,128)(2,1)}, u32[]{:S(2)}, u32[]{:S(2)}) collective-permute-start(bf16[2,4,256,768]{3,2,1,0:T(8,128)(2,1)} %get-tuple-element.139.right), channel_id=1, source_target_pairs={{0,4},{4,0},{1,5},{5,1},{2,6},{6,2},{3,7},{7,3},{8,12},{12,8},{9,1... | collective-permute-start | bytes 9437192 | tf_op jit(solution)/shard_map/ppermute | solution.py:61
  207.8 25.3 %collective-permute-start.26 = (bf16[4,256,1024]{2,1,0:T(8,128)(2,1)}, bf16[4,256,1024]{2,1,0:T(8,128)(2,1)S(1)}, u32[]{:S(2)}, u32[]{:S(2)}) collective-permute-start(bf16[4,256,1024]{2,1,0:T(8,128)(2,1)} %get-tuple-element.142.right), channel_id=1, source_target_pairs={{0,4},{4,0},{1,5},{5,1},{2,6},{6,2},{3,7},{7,3},{8,12},{12,8},{9,1... | collective-permute-start | bytes 6291464 | tf_op jit(solution)/shard_map/ppermute | solution.py:61
  208.4 24.7 %collective-permute-start.25 = (bf16[3,256,768]{2,1,0:T(8,128)(2,1)}, bf16[3,256,768]{2,1,0:T(8,128)(2,1)}, u32[]{:S(2)}, u32[]{:S(2)}) collective-permute-start(bf16[3,256,768]{2,1,0:T(8,128)(2,1)} %get-tuple-element.141.left), channel_id=1, source_target_pairs={{0,4},{4,0},{1,5},{5,1},{2,6},{6,2},{3,7},{7,3},{8,12},{12,8},{9,1... | collective-permute-start | bytes 3538952 | tf_op jit(solution)/shard_map/ppermute | solution.py:61
  214.6 27.0 %all-to-all-start.3 = ((bf16[16,32,512]{2,1,0:T(8,128)(2,1)}), bf16[16,32,512]{2,1,0:T(8,128)(2,1)}, u32[]{:S(2)}, u32[]{:S(2)}) async-start(bf16[16,32,512]{2,1,0:T(8,128)(2,1)} %bitcast.102), calls=%async_computation.3 | async-start | bytes 1048576 | tf_op jit(solution)/shard_map/all_to_all | solution.py:69
  228.3 29.7 %collective-permute-start.30 = (bf16[2,4,96,768]{3,2,1,0:T(8,128)(2,1)}, bf16[2,4,96,768]{3,2,1,0:T(8,128)(2,1)}, u32[]{:S(2)}, u32[]{:S(2)}) collective-permute-start(bf16[2,4,96,768]{3,2,1,0:T(8,128)(2,1)} %get-tuple-element.154), channel_id=1, source_target_pairs={{0,8},{8,0},{16,24},{24,16},{1,9},{9,1},{17,25},{25,17},{2,10},{10... | collective-permute-start | bytes 3538952 | tf_op jit(solution)/shard_map/ppermute | solution.py:61
  230.4 28.2 %collective-permute-start.29 = (bf16[2,4,96,768]{3,2,1,0:T(8,128)(2,1)}, bf16[2,4,96,768]{3,2,1,0:T(8,128)(2,1)}, u32[]{:S(2)}, u32[]{:S(2)}) collective-permute-start(bf16[2,4,96,768]{3,2,1,0:T(8,128)(2,1)} %get-tuple-element.153), channel_id=1, source_target_pairs={{0,16},{8,24},{16,0},{24,8},{1,17},{9,25},{17,1},{25,9},{2,18},{10... | collective-permute-start | bytes 3538952 | tf_op jit(solution)/shard_map/ppermute | solution.py:61
  278.1 32.3 %all-to-all-start.4 = ((bf16[8,3,64,512]{3,2,1,0:T(8,128)(2,1)}), bf16[8,3,64,512]{3,2,1,0:T(8,128)(2,1)S(1)}, u32[]{:S(2)}, u32[]{:S(2)}) async-start(bf16[8,3,64,512]{3,2,1,0:T(8,128)(2,1)} %pad_maximum_fusion.1), calls=%async_computation.4 | async-start | bytes 3145728 | tf_op jit(solution)/shard_map/all_to_all | solution.py:69
  286.1 23.5 %collective-permute-start.35 = (bf16[96,1536]{1,0:T(8,128)(2,1)S(1)}, bf16[96,1536]{1,0:T(8,128)(2,1)S(1)}, u32[]{:S(2)}, u32[]{:S(2)}) collective-permute-start(bf16[96,1536]{1,0:T(8,128)(2,1)S(1)} %get-tuple-element.227), channel_id=1, source_target_pairs={{0,2},{1,3},{2,0},{3,1},{4,6},{5,7},{6,4},{7,5},{8,10},{9,11},{10,... | collective-permute-start | bytes 884744 | tf_op jit(solution)/shard_map/ppermute | solution.py:61
  288.4 21.9 %collective-permute-start.36 = (bf16[96,1536]{1,0:T(8,128)(2,1)S(1)}, bf16[96,1536]{1,0:T(8,128)(2,1)}, u32[]{:S(2)}, u32[]{:S(2)}) collective-permute-start(bf16[96,1536]{1,0:T(8,128)(2,1)S(1)} %get-tuple-element.225), channel_id=1, source_target_pairs={{0,3},{1,2},{2,1},{3,0},{4,7},{5,6},{6,5},{7,4},{8,11},{9,10},{10,... | collective-permute-start | bytes 884744 | tf_op jit(solution)/shard_map/ppermute | solution.py:61
  310.3 21.5 %collective-permute-start.37 = (bf16[2,4,96,576]{3,2,1,0:T(8,128)(2,1)}, bf16[2,4,96,576]{3,2,1,0:T(8,128)(2,1)}, u32[]{:S(2)}, u32[]{:S(2)}) collective-permute-start(bf16[2,4,96,576]{3,2,1,0:T(8,128)(2,1)} %get-tuple-element.166), channel_id=1, source_target_pairs={{0,16},{8,24},{16,0},{24,8},{1,17},{9,25},{17,1},{25,9},{2,18},{10... | collective-permute-start | bytes 2654216 | tf_op jit(solution)/shard_map/ppermute | solution.py:61
  331.9 36.4 %all-to-all-start.5 = ((bf16[4,576,256]{2,1,0:T(8,128)(2,1)}), bf16[4,576,256]{2,1,0:T(8,128)(2,1)S(1)}, u32[]{:S(2)}, u32[]{:S(2)}) async-start(bf16[4,576,256]{2,1,0:T(8,128)(2,1)} %get-tuple-element.168), calls=%async_computation.5 | async-start | bytes 2359296 | tf_op jit(solution)/shard_map/all_to_all | solution.py:69
  344.4 30.1 %collective-permute-start.43 = (bf16[3,40,768]{2,1,0:T(8,128)(2,1)}, bf16[3,40,768]{2,1,0:T(8,128)(2,1)}, u32[]{:S(2)}, u32[]{:S(2)}) collective-permute-start(bf16[3,40,768]{2,1,0:T(8,128)(2,1)} %slice.159), channel_id=1, source_target_pairs={{0,8},{8,0},{16,24},{24,16},{1,9},{9,1},{17,25},{25,17},{2,10},{10... | collective-permute-start | bytes 552968 | tf_op jit(solution)/shard_map/ppermute | solution.py:61
  376.2 27.9 %collective-permute-start.44 = (bf16[3,320,768]{2,1,0:T(8,128)(2,1)}, bf16[3,320,768]{2,1,0:T(8,128)(2,1)}, u32[]{:S(2)}, u32[]{:S(2)}) collective-permute-start(bf16[3,320,768]{2,1,0:T(8,128)(2,1)} %constant_dynamic-update-slice_fusion.10.refs_5_), channel_id=1, source_target_pairs={{0,4},{4,0},{1,5},{5,1},{2,6},{6,2},{3,7},{7,3},{8,12},{12,8},{9,1... | collective-permute-start | bytes 4423688 | tf_op jit(solution)/shard_map/ppermute | solution.py:61
  390.4 23.9 %all-to-all-start.7 = ((bf16[4,112,960]{2,1,0:T(8,128)(2,1)}), bf16[4,112,960]{2,1,0:T(8,128)(2,1)S(1)}, u32[]{:S(2)}, u32[]{:S(2)}) async-start(bf16[4,112,960]{2,1,0:T(8,128)(2,1)} %pad_maximum_fusion.3), calls=%async_computation.7 | async-start | bytes 1835008 | tf_op jit(solution)/shard_map/all_to_all | solution.py:69
  (77 other events, 805.5 us)
